TPU v7x, 256 devices: a whole 4x4x8 slice. The times are simulated.
256 devices in a mesh: gx: 8 (over z), gy: 4 (over y_lo, core), gz: 8 (over y_hi, x).
Axes of the slice: x: 4, y: 4 (y_hi: 2, y_lo: 2; y = y_hi * 2 + y_lo), z: 8, core: 2. Of those that a mesh axis runs over, the one named last changes fastest.
Arguments:
- state: bfloat16 [128, 64, 16, 8, 128], P('gx', 'gy', 'gz'), may hold values from -6 to 6
- cotangent: bfloat16 [128, 64, 16, 8, 128], P('gx', 'gy', 'gz'), may hold values from -6 to 6
- counts: int32 [8], P('gz'), may hold values from 1 to 2, 12 in all
- edge_weights: bfloat16 [2, 2, 128, 128], replicated, may hold values from -0.5 to 0.5
- node_in: bfloat16 [2, 256, 128], replicated, may hold values from -0.375 to 0.375
- node_out: bfloat16 [2, 128, 128], replicated, may hold values from -0.5 to 0.5
- biases: float32 [2, 2, 128], replicated, may hold values from -4 to 4
Outputs:
- state_grad: bfloat16 [128, 64, 16, 8, 128], P('gx', 'gy', 'gz')
- edge_grads: float32 [2, 2, 128, 128], replicated
- node_in_grad: float32 [2, 256, 128], replicated
- node_out_grad: float32 [2, 128, 128], replicated
- bias_grads: float32 [2, 2, 128], replicated
Inputs may be any that keep to these rules, and one draw needn't show every extreme that they name: The counts sum to 12; index k of gz holds the element layers that follow those of smaller indices.
All inputs are finite; a program needn't handle non-finite values. No bound on the sum of `counts` on one device may be relied on, other than what follows from the above.
Results may differ from a plain program's by a relative error of at most 0.012.
The roundings to bfloat16 on the way count: a program that leaves them out, or rounds other values in their place, can miss the bound.
Values sent between devices are 32-bit elements; how exact they have to be, the bound alone decides.
A program may use at most 128 MiB of HBM per device.

v0:
```python
import math

import jax
import jax.numpy as jnp
from jax import lax
from jax.sharding import PartitionSpec as P

edge_dims = (1, 3, 5)


def with_halo(cells, sides, width):
    for axis, dim in sides:
        count = lax.axis_size(axis)
        ends = count - 1
        head = lax.slice_in_dim(cells, 0, width, axis=dim)
        tail = lax.slice_in_dim(cells, cells.shape[dim] - width, cells.shape[dim], axis=dim)
        cells = jnp.concatenate(
            [
                lax.ppermute(tail, axis, [(i, (i + 1) % count) for i in range(ends)]),
                cells,
                lax.ppermute(head, axis, [((i + 1) % count, i) for i in range(ends)]),
            ],
            axis=dim,
        )
    return cells


def slice_along(array, start, stop, dim_no):
    return lax.slice_in_dim(array, start, stop, axis=dim_no)


def matmul_rows(left, weight):
    flattened = left.reshape(-1, left.shape[-1])
    product = jnp.dot(flattened, weight, preferred_element_type=jnp.float32)
    return product.reshape(left.shape[:-1] + (weight.shape[-1],))


def cross_rows(left, right):
    return lax.dot_general(
        left.reshape(-1, left.shape[-1]),
        right.reshape(-1, right.shape[-1]),
        (((0,), (0,)), ((), ())),
        preferred_element_type=jnp.float32,
    )


def spread_diff(values, dim_no):
    zero_row = jnp.zeros_like(slice_along(values, 0, 1, dim_no))
    return jnp.concatenate([zero_row, values], dim_no) - jnp.concatenate([values, zero_row], dim_no)


def silu_slope(values):
    sig_value = jax.nn.sigmoid(values)
    return sig_value * (1.0 + values * (1.0 - sig_value))


def edges_forward(features, weight_one, weight_two, bias_edge):
    widened = features.astype(jnp.float32)
    messages = jnp.zeros(features.shape, jnp.float32)
    stored = []
    for dim_no in edge_dims:
        length = features.shape[dim_no]
        differ = (
            slice_along(widened, 1, length, dim_no) - slice_along(widened, 0, length - 1, dim_no)
        ).astype(jnp.bfloat16)
        before = matmul_rows(differ, weight_one) + bias_edge
        active = jax.nn.silu(before).astype(jnp.bfloat16)
        messages = messages + spread_diff(matmul_rows(active, weight_two), dim_no)
        stored.append((differ, before, active))
    return (messages, stored)


def edges_backward(grad_msg, stored, weight_one, weight_two):
    feat_width = grad_msg.shape[-1]
    grad_feat = jnp.zeros(grad_msg.shape, jnp.float32)
    grad_one = jnp.zeros((feat_width, feat_width), jnp.float32)
    grad_two = jnp.zeros((feat_width, feat_width), jnp.float32)
    grad_bias = jnp.zeros((feat_width,), jnp.float32)
    for dim_no, entry in zip(edge_dims, stored):
        differ, before, active = entry
        length = grad_msg.shape[dim_no]
        grad_out = (
            slice_along(grad_msg, 1, length, dim_no) - slice_along(grad_msg, 0, length - 1, dim_no)
        ).astype(jnp.bfloat16)
        grad_two = grad_two + cross_rows(active, grad_out)
        grad_pre = (matmul_rows(grad_out, weight_two.T) * silu_slope(before)).astype(jnp.bfloat16)
        grad_one = grad_one + cross_rows(differ, grad_pre)
        grad_bias = grad_bias + jnp.sum(grad_pre.astype(jnp.float32).reshape(-1, feat_width), 0)
        grad_feat = grad_feat + spread_diff(matmul_rows(grad_pre, weight_one.T), dim_no)
    return (grad_feat, grad_one, grad_two, grad_bias)


def node_forward(features, summed, weight_in, weight_out, bias_node):
    joined = jnp.concatenate([features, summed.astype(jnp.bfloat16)], -1)
    before = matmul_rows(joined, weight_in) + bias_node
    active = jax.nn.silu(before).astype(jnp.bfloat16)
    result = (features.astype(jnp.float32) + matmul_rows(active, weight_out)).astype(jnp.bfloat16)
    return (result, (joined, before, active))


def node_backward(grad_next, stored, weight_in, weight_out):
    joined, before, active = stored
    feat_width = grad_next.shape[-1]
    grad_out_w = cross_rows(active, grad_next)
    grad_pre = (matmul_rows(grad_next, weight_out.T) * silu_slope(before)).astype(jnp.bfloat16)
    grad_in_w = cross_rows(joined, grad_pre)
    grad_bias = jnp.sum(grad_pre.astype(jnp.float32).reshape(-1, feat_width), 0)
    grad_joined = matmul_rows(grad_pre, weight_in.T)
    grad_feat = grad_next.astype(jnp.float32) + grad_joined[..., :feat_width]
    return (grad_feat, grad_joined[..., feat_width:], grad_in_w, grad_out_w, grad_bias)


def couple(array, elem_dim, node_dim):
    moved = jnp.moveaxis(array, (elem_dim, node_dim), (0, 1))
    front_face = moved[:, 0]
    back_face = moved[:, -1]
    zero_face = jnp.zeros_like(front_face[:1])
    new_front = front_face + jnp.concatenate([zero_face, back_face[:-1]], 0)
    new_back = back_face + jnp.concatenate([front_face[1:], zero_face], 0)
    joined = jnp.concatenate([new_front[:, None], moved[:, 1:-1], new_back[:, None]], 1)
    return jnp.moveaxis(joined, (0, 1), (elem_dim, node_dim))


def local_couple(values, dim_no, nodes_edge):
    full_shape = values.shape
    elems_here = full_shape[dim_no] // nodes_edge
    split_shape = full_shape[:dim_no] + (elems_here, nodes_edge) + full_shape[dim_no + 1 :]
    return couple(values.reshape(split_shape), dim_no, dim_no + 1).reshape(full_shape)


def fold_rim(extended, dim_no):
    inner_len = extended.shape[dim_no] - 2
    core_rows = slice_along(extended, 1, inner_len + 1, dim_no)
    front_row = slice_along(core_rows, 0, 1, dim_no) + slice_along(extended, 0, 1, dim_no)
    back_row = slice_along(core_rows, inner_len - 1, inner_len, dim_no) + slice_along(
        extended, inner_len + 1, inner_len + 2, dim_no
    )
    return jnp.concatenate(
        [front_row, slice_along(core_rows, 1, inner_len - 1, dim_no), back_row], dim_no
    )


def on_device(state, cotangent, counts, edge_weights, node_in, node_out, biases):
    nodes_edge = state.shape[3]
    span_x = state.shape[0]
    span_y = state.shape[1]
    elems_x = span_x // nodes_edge
    elems_y = span_y // nodes_edge
    slot_count = state.shape[2]
    grid_shape = state.shape[:4]
    filled = counts[0]
    slot_ids = jnp.arange(slot_count, dtype=jnp.int32)
    node_ids = jnp.arange(nodes_edge, dtype=jnp.int32)
    live_mask = (slot_ids < filled).astype(jnp.float32)[None, None, :, None, None]

    def edge_mult(position, axis_len, elems_here):
        place = jnp.arange(elems_here * nodes_edge, dtype=jnp.int32)
        node_here = place % nodes_edge
        elem_global = position * elems_here + place // nodes_edge
        front_pair = ((node_here == 0) & (elem_global > 0)).astype(jnp.float32)
        back_pair = (
            (node_here == nodes_edge - 1) & (elem_global < elems_here * axis_len - 1)
        ).astype(jnp.float32)
        return 1.0 + front_pair + back_pair

    mult_x = edge_mult(lax.axis_index("gx"), lax.axis_size("gx"), elems_x)
    mult_y = edge_mult(lax.axis_index("gy"), lax.axis_size("gy"), elems_y)
    index_z = lax.axis_index("gz")
    size_z = lax.axis_size("gz")
    lower_mult = ((slot_ids > 0) | (index_z > 0)).astype(jnp.float32)
    upper_mult = ((slot_ids < filled - 1) | (index_z < size_z - 1)).astype(jnp.float32)
    mult_z = (
        1.0
        + (node_ids == 0).astype(jnp.float32)[None, :] * lower_mult[:, None]
        + (node_ids == nodes_edge - 1).astype(jnp.float32)[None, :] * upper_mult[:, None]
    )
    copies = (
        mult_x[:, None, None, None, None]
        * mult_y[None, :, None, None, None]
        * mult_z[None, None, :, :, None]
    )

    def couple_all(values):
        inner = local_couple(local_couple(values, 0, nodes_edge), 1, nodes_edge)
        extended = with_halo(inner, (("gx", 0), ("gy", 1)), 1)
        coupled = fold_rim(fold_rim(extended, 0), 1)
        top_faces = coupled[:, :, :, -1]
        bottom_faces = coupled[:, :, :, 0]
        top_used = lax.dynamic_index_in_dim(top_faces, filled - 1, 2, keepdims=False)
        rim_pair = jnp.stack([bottom_faces[:, :, 0], top_used], 2)
        rim_ext = with_halo(rim_pair, (("gz", 2),), 1)
        from_below = rim_ext[:, :, 0]
        from_above = rim_ext[:, :, 3]
        below_add = jnp.concatenate([from_below[:, :, None], top_faces[:, :, :-1]], 2)
        last_slot = (slot_ids == filled - 1).astype(jnp.float32)[None, None, :, None]
        above_add = (
            jnp.concatenate([bottom_faces[:, :, 1:], jnp.zeros_like(bottom_faces[:, :, :1])], 2)
            + last_slot * from_above[:, :, None]
        )
        result = jnp.concatenate(
            [
                (bottom_faces + below_add)[:, :, :, None],
                coupled[:, :, :, 1:-1],
                (top_faces + above_add)[:, :, :, None],
            ],
            3,
        )
        return result * live_mask

    def to_cells(array):
        return array.reshape(
            (elems_x, nodes_edge, elems_y, nodes_edge, slot_count, nodes_edge, array.shape[-1])
        )

    def to_grid(array):
        return array.reshape(grid_shape + (array.shape[-1],))

    features = state
    grad_next = cotangent * live_mask.astype(jnp.bfloat16)
    saved = []
    for layer_no in range(2):
        messages, edge_store = edges_forward(
            to_cells(features),
            edge_weights[layer_no, 0],
            edge_weights[layer_no, 1],
            biases[layer_no, 0],
        )
        summed = couple_all(to_grid(messages) * live_mask) / copies
        result, node_store = node_forward(
            features, summed, node_in[layer_no], node_out[layer_no], biases[layer_no, 1]
        )
        saved.append((edge_store, node_store))
        features = result
    per_layer = [None, None]
    for layer_no in (1, 0):
        edge_store, node_store = saved[layer_no]
        grad_feat, grad_sum, grad_in_w, grad_out_w, grad_node_b = node_backward(
            grad_next, node_store, node_in[layer_no], node_out[layer_no]
        )
        grad_msg = couple_all(grad_sum / copies * live_mask)
        grad_edge, grad_one, grad_two, grad_edge_b = edges_backward(
            to_cells(grad_msg), edge_store, edge_weights[layer_no, 0], edge_weights[layer_no, 1]
        )
        grad_next = (grad_feat + to_grid(grad_edge)).astype(jnp.bfloat16)
        local_terms = (
            jnp.stack([grad_one, grad_two]),
            grad_in_w,
            grad_out_w,
            jnp.stack([grad_edge_b, grad_node_b]),
        )
        per_layer[layer_no] = local_terms
    stacked = tuple(
        (jnp.stack([per_layer[0][pos_no], per_layer[1][pos_no]]) for pos_no in range(4))
    )
    stacked = lax.psum(stacked, ("gx", "gy", "gz"))
    layers_all = 3 * slot_count * size_z // 4
    nodes_all = (
        nodes_edge**3 * elems_x * lax.axis_size("gx") * elems_y * lax.axis_size("gy") * layers_all
    )
    grad_scale = 1.0 / math.sqrt(nodes_all)
    state_grad = grad_next * live_mask.astype(jnp.bfloat16)
    return (
        state_grad,
        stacked[0] * grad_scale,
        stacked[1] * grad_scale,
        stacked[2] * grad_scale,
        stacked[3] * grad_scale,
    )


def solution(mesh):
    return jax.shard_map(
        on_device,
        mesh=mesh,
        in_specs=(
            P("gx", "gy", "gz", None, None),
            P("gx", "gy", "gz", None, None),
            P("gz"),
            P(),
            P(),
            P(),
            P(),
        ),
        out_specs=(P("gx", "gy", "gz", None, None), P(), P(), P(), P()),
        check_vma=False,
    )
```

profile of v0, /device:TPU:1, one launch (start us, length us, event | category | flops | bytes accessed | tf_op | source)
XLA Modules:
  0.0 613.0 jit_solution(5968325419626531154)
XLA Ops:
  27.5 4.4 collective-permute-start
  33.2 2.4 copy_bitcast_fusion.7
  35.6 2.9 collective-permute-done.1
  40.3 4.7 collective-permute-start.2
  45.0 2.2 collective-permute-start.3
  47.4 4.4 collective-permute-done.3
  56.4 3.1 collective-permute-start.4
  63.2 4.5 collective-permute-done.5
  70.3 2.1 multiply_convert_fusion.3
  86.3 13.5 %copy.124 = f32[2,6,16,2,8,128]{5,1,0,3,4,2:T(8,128)S(1)} copy(f32[2,6,16,2,8,128]{5,3,4,2,1,0:T(2,128)S(1)} %slice.827) | data formatting | bytes 3145728 | tf_op jit(solution)/shard_map/slice | solution.py:120
  100.7 3.5 collective-permute-start.6
  106.9 5.2 collective-permute-done.7
  112.3 4.2 collective-permute-start.8
  118.6 4.4 collective-permute-done.9
  124.9 3.6 collective-permute-start.10
  133.7 3.5 collective-permute-done.11
  145.9 4.6 collective-permute-start.12
  153.1 4.1 collective-permute-done.13
  157.4 4.2 collective-permute-start.14
  164.5 3.6 collective-permute-done.15
  169.9 5.7 collective-permute-start.16
  180.8 3.2 collective-permute-done.17
  204.5 3.6 collective-permute-start.18
  211.1 3.5 collective-permute-done.19
  214.7 4.2 collective-permute-start.20
  221.6 3.8 collective-permute-done.21
  227.2 7.3 %collective-permute-start.22 = (f32[16,16,1,128]{3,1,0,2:T(8,128)S(1)}, f32[16,16,1,128]{3,1,0,2:T(8,128)S(1)}, u32[]{:S(2)}, u32[]{:S(2)}) collective-permute-start(f32[16,16,1,128]{3,1,0,2:T(8,128)S(1)} %dynamic-slice_bitcast_fusion), channel_id=1, source_target_pairs={{0,1},{1,2},{2,3},{3,4},{4,5},{5,6},{6,7},{8,9},{9,10},{10,11},{11... | collective-permute-start | bytes 393224 | tf_op jit(solution)/shard_map/ppermute | solution.py:19
  239.5 3.4 collective-permute-done.23
  258.3 84.3 %psum.31 = f32[2,2,128]{2,1,0:T(2,128)S(1)} all-reduce(f32[2,2,128]{2,1,0:T(2,128)S(1)} %pad_maximum_fusion.51), channel_id=1, replica_groups=mesh['gx'=8,'gy'=4,'gz'=8] {'gx','gy','gz'}, use_global_device_ids=true, to_apply=%region_11.12 | all-reduce | flops 512 | bytes 4096 | tf_op jit(solution)/shard_map/psum | solution.py:255
  343.2 2.8 fusion.131
  348.7 4.3 subtract_add_fusion
  354.6 246.4 %all-reduce.47.cloned.1.call-done = (f32[2,2,128,128]{3,2,1,0:T(8,128)}, f32[2,256,128]{2,1,0:T(8,128)}, f32[2,128,128]{2,1,0:T(8,128)}) async-done(((f32[2,2,128,128]{3,2,1,0:T(8,128)}, f32[2,256,128]{2,1,0:T(8,128)}, f32[2,128,128]{2,1,0:T(8,128)}), (f32[2,2,128,128]{3,2,1,0:T(8,128)}, f32[2,256,128]{2,1,0:T(8,128)}, f32[2,128,128]{2,1,0:T(8,128)})) %all-reduce.47.cloned.1.call-update) | async-done | bytes 655376 | tf_op jit(solution)/shard_map/psum | solution.py:255
  (332 shorter events, 138.7 us)
Async XLA Ops:
  7.2 593.8 %all-reduce.47.cloned.1.call-start = ((), (), s32[]{:S(2)}) async-start(), calls=%async_computation | async-start | bytes 1310720 | tf_op jit(solution)/shard_map/psum | solution.py:255
  8.9 6.6 %copy-start.14 = (bf16[2,7,2,8,2,8,128]{6,5,4,3,2,1,0:T(8,128)(2,1)}, bf16[2,7,2,8,2,8,128]{6,5,4,3,2,1,0:T(8,128)(2,1)S(1)}, u32[]{:S(2)}) copy-start(bf16[2,7,2,8,2,8,128]{6,5,4,3,2,1,0:T(8,128)(2,1)S(1)} %fusion.22) | copy-start | bytes 2752516
  12.3 7.7 %copy-start.28 = (f32[128]{0:T(128)}, f32[128]{0:T(128)S(1)}, u32[]{:S(2)}) copy-start(f32[128]{0:T(128)S(1)} %get-tuple-element.80) | copy-start | bytes 1540
  25.7 7.5 %copy-start.4 = (f32[2,16,2,8,128]{4,0,3,2,1:T(2,128)}, f32[2,16,2,8,128]{4,0,3,2,1:T(2,128)S(1)}, u32[]{:S(2)}) copy-start(f32[2,16,2,8,128]{4,0,3,2,1:T(2,128)S(1)} %copy_add_fusion.4) | copy-start | bytes 786436
  27.5 8.1 %collective-permute-start = (f32[1,16,2,8,128]{4,1,0,3,2:T(8,128)}, f32[1,16,2,8,128]{4,1,0,3,2:T(8,128)S(1)}, u32[]{:S(2)}, u32[]{:S(2)}) collective-permute-start(f32[1,16,2,8,128]{4,1,0,3,2:T(8,128)} %get-tuple-element.56), channel_id=1, source_target_pairs={{0,32},{32,64},{64,96},{96,128},{128,160},{160,192},{192,224},{1,3... | collective-permute-start | bytes 393224 | tf_op jit(solution)/shard_map/ppermute | solution.py:19
  31.8 6.7 %collective-permute-start.1 = (f32[1,16,2,8,128]{4,1,0,3,2:T(8,128)}, f32[1,16,2,8,128]{4,1,0,3,2:T(8,128)}, u32[]{:S(2)}, u32[]{:S(2)}) collective-permute-start(f32[1,16,2,8,128]{4,1,0,3,2:T(8,128)} %get-tuple-element.57), channel_id=1, source_target_pairs={{32,0},{64,32},{96,64},{128,96},{160,128},{192,160},{224,192},{33,... | collective-permute-start | bytes 393224 | tf_op jit(solution)/shard_map/ppermute | solution.py:21
  40.3 7.1 %collective-permute-start.2 = (f32[18,1,2,8,128]{4,1,0,3,2:T(1,128)}, f32[18,1,2,8,128]{4,1,0,3,2:T(1,128)S(1)}, u32[]{:S(2)}, u32[]{:S(2)}) collective-permute-start(f32[18,1,2,8,128]{4,1,0,3,2:T(1,128)} %get-tuple-element.30), channel_id=1, source_target_pairs={{0,8},{8,16},{16,24},{1,9},{9,17},{17,25},{2,10},{10,18},{18,26},{... | collective-permute-start | bytes 442376 | tf_op jit(solution)/shard_map/ppermute | solution.py:19
  45.0 6.8 %collective-permute-start.3 = (f32[18,1,2,8,128]{4,1,0,3,2:T(1,128)}, f32[18,1,2,8,128]{4,1,0,3,2:T(1,128)}, u32[]{:S(2)}, u32[]{:S(2)}) collective-permute-start(f32[18,1,2,8,128]{4,1,0,3,2:T(1,128)} %get-tuple-element.31), channel_id=1, source_target_pairs={{8,0},{16,8},{24,16},{9,1},{17,9},{25,17},{10,2},{18,10},{26,18},{... | collective-permute-start | bytes 442376 | tf_op jit(solution)/shard_map/ppermute | solution.py:21
  47.4 5.9 copy-start.5
  56.4 5.1 collective-permute-start.4
  61.6 6.1 collective-permute-start.5
  100.7 6.2 %collective-permute-start.6 = (f32[1,16,2,8,128]{4,1,0,2,3:T(8,128)S(1)}, f32[1,16,2,8,128]{4,1,0,2,3:T(8,128)S(1)}, u32[]{:S(2)}, u32[]{:S(2)}) collective-permute-start(f32[1,16,2,8,128]{4,1,0,2,3:T(8,128)S(1)} %get-tuple-element.48), channel_id=1, source_target_pairs={{0,32},{32,64},{64,96},{96,128},{128,160},{160,192},{192,224},{1,3... | collective-permute-start | bytes 393224 | tf_op jit(solution)/shard_map/ppermute | solution.py:19
  104.3 7.8 %collective-permute-start.7 = (f32[1,16,2,8,128]{4,1,0,2,3:T(8,128)S(1)}, f32[1,16,2,8,128]{4,1,0,2,3:T(8,128)S(1)}, u32[]{:S(2)}, u32[]{:S(2)}) collective-permute-start(f32[1,16,2,8,128]{4,1,0,2,3:T(8,128)S(1)} %get-tuple-element.49), channel_id=1, source_target_pairs={{32,0},{64,32},{96,64},{128,96},{160,128},{192,160},{224,192},{33,... | collective-permute-start | bytes 393224 | tf_op jit(solution)/shard_map/ppermute | solution.py:21
  112.3 6.3 %collective-permute-start.8 = (f32[18,1,2,8,128]{4,1,0,2,3:T(1,128)S(1)}, f32[18,1,2,8,128]{4,1,0,2,3:T(1,128)S(1)}, u32[]{:S(2)}, u32[]{:S(2)}) collective-permute-start(f32[18,1,2,8,128]{4,1,0,2,3:T(1,128)S(1)} %get-tuple-element.28), channel_id=1, source_target_pairs={{0,8},{8,16},{16,24},{1,9},{9,17},{17,25},{2,10},{10,18},{18,26},{... | collective-permute-start | bytes 442376 | tf_op jit(solution)/shard_map/ppermute | solution.py:19
  116.5 6.5 %collective-permute-start.9 = (f32[18,1,2,8,128]{4,1,0,2,3:T(1,128)S(1)}, f32[18,1,2,8,128]{4,1,0,2,3:T(1,128)S(1)}, u32[]{:S(2)}, u32[]{:S(2)}) collective-permute-start(f32[18,1,2,8,128]{4,1,0,2,3:T(1,128)S(1)} %get-tuple-element.29), channel_id=1, source_target_pairs={{8,0},{16,8},{24,16},{9,1},{17,9},{25,17},{10,2},{18,10},{26,18},{... | collective-permute-start | bytes 442376 | tf_op jit(solution)/shard_map/ppermute | solution.py:21
  124.9 5.6 collective-permute-start.10
  131.1 6.1 collective-permute-start.11
  145.9 7.2 %collective-permute-start.12 = (f32[1,16,2,8,128]{4,1,0,3,2:T(8,128)S(1)}, f32[1,16,2,8,128]{4,1,0,3,2:T(8,128)S(1)}, u32[]{:S(2)}, u32[]{:S(2)}) collective-permute-start(f32[1,16,2,8,128]{4,1,0,3,2:T(8,128)S(1)} %get-tuple-element.40), channel_id=1, source_target_pairs={{0,32},{32,64},{64,96},{96,128},{128,160},{160,192},{192,224},{1,3... | collective-permute-start | bytes 393224 | tf_op jit(solution)/shard_map/ppermute | solution.py:19
  150.5 6.7 %collective-permute-start.13 = (f32[1,16,2,8,128]{4,1,0,3,2:T(8,128)S(1)}, f32[1,16,2,8,128]{4,1,0,3,2:T(8,128)S(1)}, u32[]{:S(2)}, u32[]{:S(2)}) collective-permute-start(f32[1,16,2,8,128]{4,1,0,3,2:T(8,128)S(1)} %get-tuple-element.41), channel_id=1, source_target_pairs={{32,0},{64,32},{96,64},{128,96},{160,128},{192,160},{224,192},{33,... | collective-permute-start | bytes 393224 | tf_op jit(solution)/shard_map/ppermute | solution.py:21
  157.4 7.1 %collective-permute-start.14 = (f32[18,1,2,8,128]{4,1,0,3,2:T(1,128)S(1)}, f32[18,1,2,8,128]{4,1,0,3,2:T(1,128)S(1)}, u32[]{:S(2)}, u32[]{:S(2)}) collective-permute-start(f32[18,1,2,8,128]{4,1,0,3,2:T(1,128)S(1)} %get-tuple-element.24), channel_id=1, source_target_pairs={{0,8},{8,16},{16,24},{1,9},{9,17},{17,25},{2,10},{10,18},{18,26},{... | collective-permute-start | bytes 442376 | tf_op jit(solution)/shard_map/ppermute | solution.py:19
  161.6 6.5 %collective-permute-start.15 = (f32[18,1,2,8,128]{4,1,0,3,2:T(1,128)S(1)}, f32[18,1,2,8,128]{4,1,0,3,2:T(1,128)S(1)}, u32[]{:S(2)}, u32[]{:S(2)}) collective-permute-start(f32[18,1,2,8,128]{4,1,0,3,2:T(1,128)S(1)} %get-tuple-element.25), channel_id=1, source_target_pairs={{8,0},{16,8},{24,16},{9,1},{17,9},{25,17},{10,2},{18,10},{26,18},{... | collective-permute-start | bytes 442376 | tf_op jit(solution)/shard_map/ppermute | solution.py:21
  169.9 7.6 %collective-permute-start.16 = (f32[16,16,1,128]{3,1,0,2:T(8,128)S(1)}, f32[16,16,1,128]{3,1,0,2:T(8,128)S(1)}, u32[]{:S(2)}, u32[]{:S(2)}) collective-permute-start(f32[16,16,1,128]{3,1,0,2:T(8,128)S(1)} %dynamic-slice_bitcast_fusion.1), channel_id=1, source_target_pairs={{0,1},{1,2},{2,3},{3,4},{4,5},{5,6},{6,7},{8,9},{9,10},{10,11},{11... | collective-permute-start | bytes 393224 | tf_op jit(solution)/shard_map/ppermute | solution.py:19
  177.6 6.4 %collective-permute-start.17 = (f32[16,16,1,128]{3,1,0,2:T(8,128)S(1)}, f32[16,16,1,128]{3,1,0,2:T(8,128)S(1)}, u32[]{:S(2)}, u32[]{:S(2)}) collective-permute-start(f32[16,16,1,128]{3,1,0,2:T(8,128)S(1)} %get-tuple-element.70), channel_id=1, source_target_pairs={{1,0},{2,1},{3,2},{4,3},{5,4},{6,5},{7,6},{9,8},{10,9},{11,10},{12... | collective-permute-start | bytes 393224 | tf_op jit(solution)/shard_map/ppermute | solution.py:21
  204.5 6.6 %collective-permute-start.18 = (f32[1,16,2,8,128]{4,1,0,3,2:T(8,128)S(1)}, f32[1,16,2,8,128]{4,1,0,3,2:T(8,128)S(1)}, u32[]{:S(2)}, u32[]{:S(2)}) collective-permute-start(f32[1,16,2,8,128]{4,1,0,3,2:T(8,128)S(1)} %get-tuple-element.32), channel_id=1, source_target_pairs={{0,32},{32,64},{64,96},{96,128},{128,160},{160,192},{192,224},{1,3... | collective-permute-start | bytes 393224 | tf_op jit(solution)/shard_map/ppermute | solution.py:19
  208.1 6.4 %collective-permute-start.19 = (f32[1,16,2,8,128]{4,1,0,3,2:T(8,128)S(1)}, f32[1,16,2,8,128]{4,1,0,3,2:T(8,128)S(1)}, u32[]{:S(2)}, u32[]{:S(2)}) collective-permute-start(f32[1,16,2,8,128]{4,1,0,3,2:T(8,128)S(1)} %get-tuple-element.33), channel_id=1, source_target_pairs={{32,0},{64,32},{96,64},{128,96},{160,128},{192,160},{224,192},{33,... | collective-permute-start | bytes 393224 | tf_op jit(solution)/shard_map/ppermute | solution.py:21
  214.7 6.9 %collective-permute-start.20 = (f32[18,1,2,8,128]{4,1,0,3,2:T(1,128)S(1)}, f32[18,1,2,8,128]{4,1,0,3,2:T(1,128)S(1)}, u32[]{:S(2)}, u32[]{:S(2)}) collective-permute-start(f32[18,1,2,8,128]{4,1,0,3,2:T(1,128)S(1)} %get-tuple-element.22), channel_id=1, source_target_pairs={{0,8},{8,16},{16,24},{1,9},{9,17},{17,25},{2,10},{10,18},{18,26},{... | collective-permute-start | bytes 442376 | tf_op jit(solution)/shard_map/ppermute | solution.py:19
  219.0 6.5 %collective-permute-start.21 = (f32[18,1,2,8,128]{4,1,0,3,2:T(1,128)S(1)}, f32[18,1,2,8,128]{4,1,0,3,2:T(1,128)S(1)}, u32[]{:S(2)}, u32[]{:S(2)}) collective-permute-start(f32[18,1,2,8,128]{4,1,0,3,2:T(1,128)S(1)} %get-tuple-element.23), channel_id=1, source_target_pairs={{8,0},{16,8},{24,16},{9,1},{17,9},{25,17},{10,2},{18,10},{26,18},{... | collective-permute-start | bytes 442376 | tf_op jit(solution)/shard_map/ppermute | solution.py:21
  227.2 9.2 %collective-permute-start.22 = (f32[16,16,1,128]{3,1,0,2:T(8,128)S(1)}, f32[16,16,1,128]{3,1,0,2:T(8,128)S(1)}, u32[]{:S(2)}, u32[]{:S(2)}) collective-permute-start(f32[16,16,1,128]{3,1,0,2:T(8,128)S(1)} %dynamic-slice_bitcast_fusion), channel_id=1, source_target_pairs={{0,1},{1,2},{2,3},{3,4},{4,5},{5,6},{6,7},{8,9},{9,10},{10,11},{11... | collective-permute-start | bytes 393224 | tf_op jit(solution)/shard_map/ppermute | solution.py:19
  236.5 6.4 %collective-permute-start.23 = (f32[16,16,1,128]{3,1,0,2:T(8,128)S(1)}, f32[16,16,1,128]{3,1,0,2:T(8,128)S(1)}, u32[]{:S(2)}, u32[]{:S(2)}) collective-permute-start(f32[16,16,1,128]{3,1,0,2:T(8,128)S(1)} %get-tuple-element.68), channel_id=1, source_target_pairs={{1,0},{2,1},{3,2},{4,3},{5,4},{6,5},{7,6},{9,8},{10,9},{11,10},{12... | collective-permute-start | bytes 393224 | tf_op jit(solution)/shard_map/ppermute | solution.py:21
  244.2 11.2 %copy-start.22 = (bf16[2,7,2,8,2,8,128]{6,5,4,3,2,1,0:T(8,128)(2,1)}, bf16[2,7,2,8,2,8,128]{6,5,4,3,2,1,0:T(8,128)(2,1)S(1)}, u32[]{:S(2)}) copy-start(bf16[2,7,2,8,2,8,128]{6,5,4,3,2,1,0:T(8,128)(2,1)S(1)} %fusion.16) | copy-start | bytes 2752516
  342.6 3.4 copy-start.23
  348.7 4.4 copy-start.3
  (34 other events, 49.8 us)
Sparse Core Ops, SparseCore 0:
  348.9 252.0 all-reduce.46
where the time goes:
time: 616 us; the launch traced here: 613 us
  waiting for transfers between devices  299 us (49%)
  blocking collectives  84.3 us (14%)
  starting transfers between devices  72.2 us (12%)
  other arithmetic  53.6 us (9%)
  matrix products  43.4 us (7%)
  local copies, waits for them, and re-layouts  43.2 us (7%)
  between operations  16.8 us (3%)
    psum x1, waiting for transfers between devices, on_device(): stacked = lax.psum(stacked, ('gx', 'gy', 'gz'))  246 us
    psum x1, blocking collectives, on_device(): stacked = lax.psum(stacked, ('gx', 'gy', 'gz'))  84.3 us
    ppermute x12, starting transfers between devices, with_halo(): lax.ppermute(tail, axis, [(i, (i + 1) % count) for i in range(ends)])  53.2 us
    ppermute x12, waiting for transfers between devices, with_halo(): lax.ppermute(head, axis, [((i + 1) % count, i) for i in range(ends)])  46.5 us
    dot_general x31, matrix products, matmul_rows(): product = jnp.dot(flattened, weight, preferred_element_type=jnp.float32)  31.6 us
    ppermute x12, starting transfers between devices, with_halo(): lax.ppermute(head, axis, [((i + 1) % count, i) for i in range(ends)])  18.9 us
    slice x12, local copies, waits for them, and re-layouts, couple(): moved[:, 1:-1]  17.8 us
    unnamed x82, local copies, waits for them, and re-layouts  12.7 us
  transfers between devices with their start and end apart: 25, of which 21 were waited for; matrix products, arithmetic and copies ran while one was open for 3% of the time, Pallas kernels for 0%

commit v1 on v0

v1 whole, which is shorter than its diff:
```python
import functools
import math

import jax
import jax.numpy as jnp
from jax import lax
from jax.experimental import pallas as pl
from jax.experimental.pallas import tpu as pltpu
from jax.sharding import PartitionSpec as P

F32 = jnp.float32
BF16 = jnp.bfloat16
H = 128
ROWS = 768
MESH = pl.DeviceIdType.MESH


def mm(a, b):
    return jnp.dot(a, b, preferred_element_type=F32)


def mm_rows(a, b):
    return lax.dot_general(a, b, (((0,), (0,)), ((), ())), preferred_element_type=F32)


def act(pre):
    sig = 0.5 * jnp.tanh(0.5 * pre) + 0.5
    value = pre * sig
    return value, sig + value - value * sig


def flat(x):
    return x.reshape(256, x.shape[-1])


def kernel(
    sizes,
    scale,
    state,
    cotangent,
    counts,
    edge_w,
    node_in,
    node_out,
    biases,
    state_grad,
    edge_grads,
    node_in_grad,
    node_out_grad,
    bias_grads,
    w_first,
    w_agg,
    w_out_t,
    w_in_t,
    w_two_t,
    w_one_t,
    h_one,
    g_mid,
    pre_a,
    pre_n,
    field,
    dh,
    slope_x,
    slope_y,
    slope_z,
    slope_n,
    spread,
    agg,
    active,
    inv_yz,
    carry,
    pbuf,
    dbuf,
    hilo,
    bias_acc,
    gbuf,
    x_in,
    y_in,
    z_out,
    z_in,
    red_y,
    sum_y,
    red_x,
    sum_x,
    red_z,
    sum_z,
    gat_x,
    gat_y,
    ex_send,
    ex_recv,
    ar_send,
    ar_recv,
):
    n_x, n_y, n_z = sizes
    i_x, i_y, i_z = lax.axis_index("gx"), lax.axis_index("gy"), lax.axis_index("gz")
    here = {"gx": i_x, "gy": i_y, "gz": i_z}
    size = {"gx": n_x, "gy": n_y, "gz": n_z}

    def peer(axis, d):
        return lax.rem(here[axis] + d, size[axis])

    def at_axis(axis, d):
        q = peer(axis, d)
        return tuple(q if name == axis else here[name] for name in ("gx", "gy", "gz"))

    barrier = pltpu.get_barrier_semaphore()
    for axis in ("gx", "gy", "gz"):
        for d in range(1, size[axis]):
            pl.semaphore_signal(barrier, inc=1, device_id=at_axis(axis, d), device_id_type=MESH)
    pl.semaphore_wait(barrier, n_x + n_y + n_z - 3)

    def flag(cond):
        return jnp.where(cond, 1.0, 0.0).astype(F32)

    live = flag(counts[0] > 1)
    left = {axis: flag(here[axis] > 0) for axis in here}
    right = {axis: flag(here[axis] < size[axis] - 1) for axis in here}

    sk = lax.broadcasted_iota(jnp.int32, (16, H), 0)
    one = jnp.ones((16, H), F32)
    zero = jnp.zeros((16, H), F32)
    row_live = jnp.where(sk < 8, one, one * live)
    not_top = jnp.where((sk == 7) | (sk == 15), zero, one)
    bottom = jnp.where(sk == 0, one, zero)
    top = jnp.where(sk == 7, one * (1.0 - live), jnp.where(sk == 15, one * live, zero))
    mult_z = (
        one
        + jnp.where(sk == 0, one * left["gz"], zero)
        + jnp.where(sk == 8, one, zero)
        + jnp.where(sk == 7, one * jnp.maximum(live, right["gz"]), zero)
        + jnp.where(sk == 15, one * right["gz"], zero)
    )
    for y in range(16):
        mult_y = {0: left["gy"], 7: 1.0, 8: 1.0, 15: right["gy"]}.get(y, 0.0)
        inv_yz[y] = 1.0 / (mult_z * (1.0 + mult_y))

    def inv_x(p):
        extra = (
            flag(p == 0) * left["gx"]
            + flag((p == 7) | (p == 8))
            + flag(p == 15) * right["gx"]
        )
        return 1.0 - 0.5 * extra

    def turn(w):
        return w.astype(F32).T.astype(BF16)

    for l in range(2):
        w_first[l] = jnp.concatenate([edge_w[l, 0], node_in[l, :H]], 1)
        w_agg[l] = node_in[l, H:]
        w_out_t[l] = turn(node_out[l])
        w_in_t[l] = jnp.concatenate([turn(node_in[l, :H]), turn(node_in[l, H:])], 1)
        two_t = turn(edge_w[l, 1])
        w_two_t[l] = jnp.concatenate([two_t, two_t], 0)
        w_one_t[l] = turn(edge_w[l, 0])
    gbuf[...] = jnp.zeros_like(gbuf)
    bias_acc[...] = jnp.zeros_like(bias_acc)

    def roll_up(x):
        return pltpu.roll(x.reshape(16, 8, H), 7, 1).reshape(8, 16, H)

    def roll_down(x):
        return pltpu.roll(x.reshape(16, 8, H), 1, 1).reshape(8, 16, H)

    def spread_y(u):
        pad = jnp.zeros((1, 16, H), F32)
        return jnp.concatenate([pad, u], 0) - jnp.concatenate([u, pad], 0)

    def put_first(l, p, h_plane):
        both = mm(h_plane, w_first[l])
        pre_a[p] = both[:, :H].reshape(16, 16, H)
        pre_n[p] = both[:, H:].reshape(16, 16, H)

    def put_field(p, r):
        r = r.reshape(16, 16, H) * row_live
        low, high = r[:, :8], r[:, 8:]
        k = lax.broadcasted_iota(jnp.int32, (16, 8, H), 1)
        none = jnp.zeros((16, 8, H), F32)
        low2 = low + jnp.where(k == 7, pltpu.roll(high, 7, 1), none)
        high2 = high + jnp.where(k == 0, pltpu.roll(low, 1, 1), none)
        r = jnp.concatenate([low2, high2], 1)
        joint = r[7:8] + r[8:9]
        field[p] = jnp.concatenate([r[:7], joint, joint, r[9:]], 0)

    def messages(l):
        carry[...] = jnp.zeros_like(carry)
        bias = biases[l, 0:1]

        def step(p, _):
            nxt = jnp.minimum(p + 1, 15)
            inner = 1.0 - flag(lax.rem(p, 8) == 7)
            for e in (0, 1):
                ys = slice(8 * e, 8 * e + 8)
                mine = pre_a[p, ys]
                biased = mine - bias
                ux, sx = act(pre_a[nxt, ys] - biased)
                ux = ux * inner
                slope_x[l, p, ys] = sx * inner
                total = carry[ys] - ux
                carry[ys] = ux
                uy, sy = act(mine[1:] - biased[:7])
                slope_y[l, p, 8 * e : 8 * e + 7] = sy
                total = total + spread_y(uy)
                uz, sz = act(roll_up(mine) - biased)
                uz = uz * not_top
                slope_z[l, p, ys] = sz * not_top
                total = total + roll_down(uz) - uz
                spread[l, p, ys] = total.astype(BF16)
            put_field(p, mm(flat(spread[l, p]), edge_w[l, 1]))
            return 0

        lax.fori_loop(0, 16, step, 0)

    def join_x():
        joint = field[7] + field[8]
        field[7] = joint
        field[8] = joint

    def remote(src, dst, n, axis, d, send, recv):
        return pltpu.make_async_remote_copy(
            src_ref=src,
            dst_ref=dst,
            send_sem=send.at[n],
            recv_sem=recv.at[n],
            device_id=at_axis(axis, d),
            device_id_type=MESH,
        )

    def exchange(e):
        join_x()
        sends = [
            remote(field.at[0], x_in.at[e, 1], 6 * e, "gx", n_x - 1, ex_send, ex_recv),
            remote(field.at[15], x_in.at[e, 0], 6 * e + 1, "gx", 1, ex_send, ex_recv),
        ]
        for s in sends:
            s.start()
        for s in sends:
            s.wait()
        field[0] = field[0] + x_in[e, 0] * left["gx"]
        field[15] = field[15] + x_in[e, 1] * right["gx"]
        sends = [
            remote(field.at[:, 0], y_in.at[e, 1], 6 * e + 2, "gy", n_y - 1, ex_send, ex_recv),
            remote(field.at[:, 15], y_in.at[e, 0], 6 * e + 3, "gy", 1, ex_send, ex_recv),
        ]
        for s in sends:
            s.start()
        for s in sends:
            s.wait()

        def edge(p, _):
            field[p, 0] = field[p, 0] + y_in[e, 0, p] * left["gy"]
            field[p, 15] = field[p, 15] + y_in[e, 1, p] * right["gy"]
            z_out[e, 0, p] = field[p, :, 0, :]
            z_out[e, 1, p] = field[p, :, 7, :] * (1.0 - live) + field[p, :, 15, :] * live
            return 0

        lax.fori_loop(0, 16, edge, 0)
        sends = [
            remote(z_out.at[e, 0], z_in.at[e, 1], 6 * e + 4, "gz", n_z - 1, ex_send, ex_recv),
            remote(z_out.at[e, 1], z_in.at[e, 0], 6 * e + 5, "gz", 1, ex_send, ex_recv),
        ]
        for s in sends:
            s.start()
        for s in sends:
            s.wait()

    bottom_in = bottom * left["gz"]
    top_in = top * right["gz"]

    def summed(e, p):
        below = z_in[e, 0, p][:, None, :]
        above = z_in[e, 1, p][:, None, :]
        return field[p] + below * bottom_in + above * top_in

    def node(l, e, p, h_plane):
        a = (summed(e, p) * (inv_yz[...] * inv_x(p))).astype(BF16)
        agg[l, p] = a
        pre = mm(flat(a), w_agg[l]) + flat(pre_n[p]) + biases[l, 1:2]
        v, slope = act(pre)
        v = v.astype(BF16)
        active[l, p] = v.reshape(16, 16, H)
        return v, slope

    def node_back(l, p, h_plane, g, slope):
        dpn = mm(g, w_out_t[l]) * slope
        bias_acc[l, 1] = bias_acc[l, 1] + jnp.sum(dpn.reshape(16, 16, H), 0)
        dpn = dpn.astype(BF16)
        gbuf[l, 512:640] += mm_rows(flat(active[l, p]), g)
        gbuf[l, 256:384] += mm_rows(h_plane, dpn)
        gbuf[l, 384:512] += mm_rows(flat(agg[l, p]), dpn)
        dx = mm(dpn, w_in_t[l])
        dh[p] = (g.astype(F32) + dx[:, :H]).reshape(16, 16, H)
        r = dx[:, H:].reshape(16, 16, H) * (inv_yz[...] * inv_x(p))
        put_field(p, r)

    def edge_first(l, e):
        def step(p, _):
            dr = flat(summed(e, p) * row_live)
            hi = dr.astype(BF16)
            lo = (dr - hi.astype(F32)).astype(BF16)
            pair = jnp.concatenate([hi, lo], 1)
            pre_a[p] = mm(pair, w_two_t[l]).reshape(16, 16, H)
            both = mm_rows(flat(spread[l, p]), pair)
            gbuf[l, 128:256] += both[:, :H] + both[:, H:]
            return 0

        lax.fori_loop(0, 16, step, 0)

    def edge_back(l, p, h_plane):
        nxt = jnp.minimum(p + 1, 15)
        for e in (0, 1):
            ys = slice(8 * e, 8 * e + 8)
            mine = pre_a[p, ys]
            dx = (pre_a[nxt, ys] - mine) * slope_x[l, p, ys]
            total = carry[ys] - dx
            carry[ys] = dx
            dy = (mine[1:] - mine[:7]) * slope_y[l, p, 8 * e : 8 * e + 7]
            total = total + spread_y(dy)
            dz = (roll_up(mine) - mine) * slope_z[l, p, ys]
            total = total + roll_down(dz) - dz
            bias_acc[l, 0] = bias_acc[l, 0] + (
                jnp.sum(dx, 0) + jnp.sum(dy, 0) + jnp.sum(dz, 0)
            )
            pbuf[ys] = total.astype(BF16)
        back = flat(pbuf[...])
        gbuf[l, 0:128] += mm_rows(h_plane, back)
        return (flat(dh[p]) + mm(back, w_one_t[l])).astype(BF16)

    def start_all(copies):
        for c in copies:
            c.start()
        return copies

    def wait_all(copies):
        for c in copies:
            c.wait()

    part_y, part_x = ROWS // n_y, ROWS // n_y // n_x
    first_z = n_y - 1 + n_x - 1
    first_gx = first_z + n_z - 1
    first_gy = first_gx + n_x - 1

    def ar_one(l):
        return start_all([
            remote(
                gbuf.at[l, pl.ds(pl.multiple_of(peer("gy", d) * part_y, 8), part_y)],
                red_y.at[l, d - 1], d - 1, "gy", d, ar_send.at[l], ar_recv.at[l],
            )
            for d in range(1, n_y)
        ])

    def ar_two(l, sent):
        wait_all(sent)
        total = gbuf[l, pl.ds(pl.multiple_of(i_y * part_y, 8), part_y)]
        for d in range(1, n_y):
            total = total + red_y[l, d - 1]
        sum_y[l] = total
        return start_all([
            remote(
                sum_y.at[l, pl.ds(pl.multiple_of(peer("gx", d) * part_x, 8), part_x)],
                red_x.at[l, d - 1], n_y - 2 + d, "gx", d, ar_send.at[l], ar_recv.at[l],
            )
            for d in range(1, n_x)
        ])

    def ar_three(l, sent):
        wait_all(sent)
        total = sum_y[l, pl.ds(pl.multiple_of(i_x * part_x, 8), part_x)]
        for d in range(1, n_x):
            total = total + red_x[l, d - 1]
        sum_x[l] = total
        red_z[l, i_z] = total
        return start_all([
            remote(
                sum_x.at[l], red_z.at[l, i_z], first_z + d - 1, "gz", d,
                ar_send.at[l], ar_recv.at[l],
            )
            for d in range(1, n_z)
        ])

    def ar_four(l, sent):
        wait_all(sent)
        total = red_z[l, 0]
        for d in range(1, n_z):
            total = total + red_z[l, d]
        total = total * scale
        sum_z[l] = total
        gat_x[l, pl.ds(pl.multiple_of(i_x * part_x, 8), part_x)] = total
        return start_all([
            remote(
                sum_z.at[l], gat_x.at[l, pl.ds(pl.multiple_of(i_x * part_x, 8), part_x)],
                first_gx + d - 1, "gx", d, ar_send.at[l], ar_recv.at[l],
            )
            for d in range(1, n_x)
        ])

    def ar_five(l, sent):
        wait_all(sent)
        gat_y[l, pl.ds(pl.multiple_of(i_y * part_y, 8), part_y)] = gat_x[l]
        return start_all([
            remote(
                gat_x.at[l], gat_y.at[l, pl.ds(pl.multiple_of(i_y * part_y, 8), part_y)],
                first_gy + d - 1, "gy", d, ar_send.at[l], ar_recv.at[l],
            )
            for d in range(1, n_y)
        ])

    def ar_last(l, sent):
        wait_all(sent)
        edge_grads[l, 0] = gat_y[l, 0:128]
        edge_grads[l, 1] = gat_y[l, 128:256]
        node_in_grad[l] = gat_y[l, 256:512]
        node_out_grad[l] = gat_y[l, 512:640]
        bias_grads[l] = gat_y[l, 640:642]

    def finish_bias(l):
        gbuf[l, 640:641] = jnp.sum(bias_acc[l, 0], 0, keepdims=True)
        gbuf[l, 641:642] = jnp.sum(bias_acc[l, 1], 0, keepdims=True)

    def first(p, _):
        put_first(0, p, flat(state[p]))
        return 0

    lax.fori_loop(0, 16, first, 0)
    messages(0)
    exchange(0)

    def middle(p, _):
        h_plane = flat(state[p])
        v, slope = node(0, 0, p, h_plane)
        slope_n[p] = slope.reshape(16, 16, H)
        nxt = (h_plane.astype(F32) + mm(v, node_out[0])).astype(BF16)
        h_one[p] = nxt.reshape(16, 16, H)
        put_first(1, p, nxt)
        return 0

    lax.fori_loop(0, 16, middle, 0)
    messages(1)
    exchange(1)

    def last(p, _):
        h_plane = flat(h_one[p])
        v, slope = node(1, 1, p, h_plane)
        g = flat((cotangent[p].astype(F32) * row_live).astype(BF16))
        node_back(1, p, h_plane, g, slope)
        return 0

    lax.fori_loop(0, 16, last, 0)
    exchange(2)
    edge_first(1, 2)
    carry[...] = jnp.zeros_like(carry)

    def turnover(p, _):
        g = edge_back(1, p, flat(h_one[p]))
        node_back(0, p, flat(state[p]), g, flat(slope_n[p]))
        return 0

    lax.fori_loop(0, 16, turnover, 0)
    finish_bias(1)
    sent = ar_one(1)
    exchange(3)
    sent = ar_two(1, sent)
    edge_first(0, 3)
    sent = ar_three(1, sent)
    carry[...] = jnp.zeros_like(carry)

    def final(p, _):
        g = edge_back(0, p, flat(state[p]))
        state_grad[p] = g.reshape(16, 16, H)
        return 0

    lax.fori_loop(0, 16, final, 0)
    finish_bias(0)
    sent0 = ar_one(0)
    sent = ar_four(1, sent)
    sent0 = ar_two(0, sent0)
    sent = ar_five(1, sent)
    sent0 = ar_three(0, sent0)
    ar_last(1, sent)
    sent0 = ar_four(0, sent0)
    sent0 = ar_five(0, sent0)
    ar_last(0, sent0)


def on_device(sizes, state, cotangent, counts, edge_weights, node_in, node_out, biases):
    n_x, n_y, n_z = sizes
    shape = state.shape
    nodes = (shape[0] * n_x) * (shape[1] * n_y) * (3 * shape[2] * n_z // 4) * shape[3]
    planes = (shape[0], shape[1], shape[2] * shape[3], H)
    part_y, part_x = ROWS // n_y, ROWS // n_y // n_x
    n_ar = 2 * (n_x - 1) + 2 * (n_y - 1) + n_z - 1
    vmem = pl.BlockSpec(memory_space=pltpu.VMEM)
    scratch = [
        pltpu.VMEM((2, H, 2 * H), BF16),
        pltpu.VMEM((2, H, H), BF16),
        pltpu.VMEM((2, H, H), BF16),
        pltpu.VMEM((2, H, 2 * H), BF16),
        pltpu.VMEM((2, 2 * H, H), BF16),
        pltpu.VMEM((2, H, H), BF16),
        pltpu.VMEM(planes, BF16),
        pltpu.VMEM((8, H), BF16),
        pltpu.VMEM(planes, F32),
        pltpu.VMEM(planes, F32),
        pltpu.VMEM(planes, F32),
        pltpu.VMEM(planes, F32),
        pltpu.VMEM((2,) + planes, F32),
        pltpu.VMEM((2,) + planes, F32),
        pltpu.VMEM((2,) + planes, F32),
        pltpu.VMEM(planes, F32),
        pltpu.VMEM((2,) + planes, BF16),
        pltpu.VMEM((2,) + planes, BF16),
        pltpu.VMEM((2,) + planes, BF16),
        pltpu.VMEM(planes[1:], F32),
        pltpu.VMEM(planes[1:], F32),
        pltpu.VMEM(planes[1:], BF16),
        pltpu.VMEM((8, H), BF16),
        pltpu.VMEM((8, H), BF16),
        pltpu.VMEM((2, 2, 16, H), F32),
        pltpu.VMEM((2, ROWS, H), F32),
        pltpu.VMEM((4, 2) + planes[1:], F32),
        pltpu.VMEM((4, 2, 16, 16, H), F32),
        pltpu.VMEM((4, 2, 16, 16, H), F32),
        pltpu.VMEM((4, 2, 16, 16, H), F32),
        pltpu.VMEM((2, n_y - 1, part_y, H), F32),
        pltpu.VMEM((2, part_y, H), F32),
        pltpu.VMEM((2, n_x - 1, part_x, H), F32),
        pltpu.VMEM((2, part_x, H), F32),
        pltpu.VMEM((2, n_z, part_x, H), F32),
        pltpu.VMEM((2, part_x, H), F32),
        pltpu.VMEM((2, part_y, H), F32),
        pltpu.VMEM((2, ROWS, H), F32),
        pltpu.SemaphoreType.DMA((24,)),
        pltpu.SemaphoreType.DMA((24,)),
        pltpu.SemaphoreType.DMA((2, n_ar)),
        pltpu.SemaphoreType.DMA((2, n_ar)),
    ]
    outs = pl.pallas_call(
        functools.partial(kernel, sizes, 1.0 / math.sqrt(nodes)),
        out_shape=(
            jax.ShapeDtypeStruct(planes, BF16),
            jax.ShapeDtypeStruct((2, 2, H, H), F32),
            jax.ShapeDtypeStruct((2, 2 * H, H), F32),
            jax.ShapeDtypeStruct((2, H, H), F32),
            jax.ShapeDtypeStruct((2, 2, H), F32),
        ),
        in_specs=[vmem, vmem, pl.BlockSpec(memory_space=pltpu.SMEM), vmem, vmem, vmem, vmem],
        out_specs=(vmem,) * 5,
        scratch_shapes=scratch,
        compiler_params=pltpu.CompilerParams(
            collective_id=0, has_side_effects=True, vmem_limit_bytes=66_000_000
        ),
        name="layers",
    )(
        state.reshape(planes),
        cotangent.reshape(planes),
        counts,
        edge_weights,
        node_in,
        node_out,
        biases,
    )
    return (outs[0].reshape(shape),) + tuple(outs[1:])


def solution(mesh):
    sizes = tuple(mesh.shape[name] for name in ("gx", "gy", "gz"))
    grid = P("gx", "gy", "gz", None, None)
    return jax.shard_map(
        functools.partial(on_device, sizes),
        mesh=mesh,
        in_specs=(grid, grid, P("gz"), P(), P(), P(), P()),
        out_specs=(grid, P(), P(), P(), P()),
        check_vma=False,
    )
```

time: 616 us -> 161 us (0.26)
  waiting for transfers between devices: 299 us -> 0 us
  Pallas kernels: 0 us -> 154 us
  blocking collectives: 84.3 us -> 0 us
  starting transfers between devices: 72.2 us -> 0 us
  other arithmetic: 53.6 us -> 0 us
  matrix products: 43.4 us -> 0 us
  local copies, waits for them, and re-layouts: 43.2 us -> 5.75 us
  between operations: 16.8 us -> 1.3 us
    psum x1 -> x0, waiting for transfers between devices: 246 us -> none  [on_device(): stacked = lax.psum(stacked, ('gx', 'gy', 'gz'))]
    pallas_call x0 -> x1, Pallas kernels: none -> 154 us  [on_device(): pl.pallas_call(functools.partial(kernel, sizes, 1.0 / math.sqrt(nodes)),...]
    psum x1 -> x0, blocking collectives: 84.3 us -> none  [on_device(): stacked = lax.psum(stacked, ('gx', 'gy', 'gz'))]
    ppermute x24 -> x0, starting transfers between devices: 72.1 us -> none  [the longest x12 53.2 us: with_halo(): lax.ppermute(tail, axis, [(i, (i + 1) % count) for i in range(ends)])]
    ppermute x24 -> x0, waiting for transfers between devices: 53.1 us -> none  [the longest x12 46.5 us: with_halo(): lax.ppermute(head, axis, [((i + 1) % count, i) for i in range(ends)])]
    dot_general x47 -> x0, matrix products: 43.4 us -> none  [the longest x31 31.6 us: matmul_rows(): product = jnp.dot(flattened, weight, preferred_element_type=jnp.float32)]
    slice x48 -> x0, local copies, waits for them, and re-layouts: 25.5 us -> none  [the longest x12 17.8 us: couple(): moved[:, 1:-1]]
    add x31 -> x0, other arithmetic: 12.6 us -> none  [the longest x2 4.97 us: edges_backward(): grad_feat + spread_diff(matmul_rows(grad_pre, weight_one.T), dim_no)]
  transfers between devices with their start and end apart: 25 -> 0, of which waited for: 21 -> 0; matrix products, arithmetic and copies ran while one was open for 3% -> 0% of each run, Pallas kernels for 0% -> 0%
where the time goes in v1:
time: 161 us
  Pallas kernels  154 us (96%)
  local copies, waits for them, and re-layouts  5.75 us (4%)
    pallas_call x1, Pallas kernels, on_device(): pl.pallas_call(functools.partial(kernel, sizes, 1.0 / math.sqrt(nodes)),...  154 us
    unnamed x13, local copies, waits for them, and re-layouts  5.75 us

profile of v1, /device:TPU:1, one launch (start us, length us, event | category | flops | bytes accessed | tf_op | source)
XLA Modules:
  0.0 161.0 jit_solution(2462633775105813356)
XLA Ops:
  1.3 153.9 %layers.1 = (bf16[16,16,16,128]{3,2,1,0:T(8,128)(2,1)}, f32[2,2,128,128]{3,2,1,0:T(8,128)}, f32[2,256,128]{2,1,0:T(8,128)}, f32[2,128,128]{2,1,0:T(8,128)}, f32[2,2,128]{2,1,0:T(2,128)}) custom-call(bf16[16,16,16,128]{3,2,1,0:T(8,128)(2,1)} %bitcast.3, bf16[16,16,16,128]{3,2,1,0:T(8,128)(2,1)} %bitcast.4, s32[1]{0:T(128)S(6)} %copy.17.counts, ...), custom_call_target="tpu_custom_call" | custom-call | tf_op jit(solution)/shard_map/layers/pallas_call | solution.py:537
  155.2 0.0 copy-start.1
  155.2 2.5 %copy.18 = bf16[16,16,2,8,128]{4,3,2,1,0:T(8,128)(2,1)} copy(bf16[16,16,2,8,128]{4,3,2,1,0:T(8,128)(2,1)} %bitcast.5) | data formatting | bytes 2097152
  157.7 0.0 copy-done.1
  157.7 0.0 copy-start
  157.7 0.7 copy.19
  158.4 0.3 copy-done
  158.7 0.0 copy-start.2
  158.7 0.7 copy.20
  159.4 0.3 copy-done.2
  159.7 0.0 copy-start.3
  159.7 0.7 copy.21
  160.4 0.0 copy-done.3
  160.4 0.6 copy.22
Async XLA Ops:
  155.2 2.5 %copy-start.1 = (f32[2,2,128,128]{3,2,1,0:T(8,128)S(1)}, f32[2,2,128,128]{3,2,1,0:T(8,128)}, u32[]{:S(2)}) copy-start(f32[2,2,128,128]{3,2,1,0:T(8,128)} %get-tuple-element.21) | copy-start | bytes 786436
  157.7 1.0 copy-start
  158.7 1.0 copy-start.2
  159.7 0.7 copy-start.3

commit v2 on v1

v2 whole, which is shorter than its diff:
```python
import functools
import math

import jax
import jax.numpy as jnp
from jax import lax
from jax.experimental import pallas as pl
from jax.experimental.pallas import tpu as pltpu
from jax.sharding import PartitionSpec as P

F32 = jnp.float32
BF16 = jnp.bfloat16
H = 128
MESH = pl.DeviceIdType.MESH
AXES = ("gx", "gy", "gz")
UNITS = (768, 768, 256)
GROUPS = ((0, 1), (1, 5), (5, 8))


def mm(a, b):
    return jnp.dot(a, b, preferred_element_type=F32)


def mm_rows(a, b):
    return lax.dot_general(a, b, (((0,), (0,)), ((), ())), preferred_element_type=F32)


def act(x):
    t = jnp.tanh(x)
    m = x * t
    return x + m, (1.0 + t) * ((1.0 + x) - m)


def flat(x):
    return x.reshape(-1, x.shape[-1])


def kernel(sizes, scale, *refs):
    (
        state, cotangent, counts, edge_w, node_in, node_out, biases,
        state_grad, edge_grads, node_in_grad, node_out_grad, bias_grads,
        w_first, w_agg, w_out_t, w_in_t, w_two_t, w_one_t, half_bias,
        h_one, g_now, d_now, p_now, pre_a, pre_n, field, dh,
        slope_x, slope_y, slope_z, slope_n, spread, agg, active, inv_yz, carry, bias_acc,
        x_in, y_out, y_in, z_out, z_in, yz_out, yz_in, ex_send, ex_recv,
    ) = refs[:46]
    units = [refs[46 + 11 * u : 57 + 11 * u] for u in range(3)]
    n_x, n_y, n_z = sizes
    i_x, i_y, i_z = (lax.axis_index(name) for name in AXES)
    here = dict(zip(AXES, (i_x, i_y, i_z)))
    size = dict(zip(AXES, sizes))

    def peer(axis, d):
        return lax.rem(here[axis] + d, size[axis])

    def device(**moves):
        return tuple(peer(a, moves[a] % size[a]) if a in moves else here[a] for a in AXES)

    barrier = pltpu.get_barrier_semaphore()
    partners = [device(**{a: d}) for a in AXES for d in range(1, size[a])]
    partners += [device(gy=dy, gz=dz) for dy in (-1, 1) for dz in (-1, 1)]
    for q in partners:
        pl.semaphore_signal(barrier, inc=1, device_id=q, device_id_type=MESH)
    pl.semaphore_wait(barrier, len(partners))

    def flag(cond):
        return jnp.where(cond, 1.0, 0.0).astype(F32)

    live = flag(counts[0] > 1)
    left = {a: flag(here[a] > 0) for a in AXES}
    right = {a: flag(here[a] < size[a] - 1) for a in AXES}

    sk = lax.broadcasted_iota(jnp.int32, (16, H), 0)
    one = jnp.ones((16, H), F32)
    zero = jnp.zeros((16, H), F32)
    row_live = jnp.where(sk < 8, one, one * live)
    not_top = jnp.where((sk == 7) | (sk == 15), zero, one)
    bottom = jnp.where(sk == 0, one, zero)
    top = jnp.where(sk == 7, one * (1.0 - live), jnp.where(sk == 15, one * live, zero))
    bottom_in = bottom * left["gz"]
    top_in = top * right["gz"]
    first_y = bottom * left["gy"]
    last_y = jnp.where(sk == 15, one * right["gy"], zero)
    mult_z = (
        one
        + jnp.where(sk == 0, one * left["gz"], zero)
        + jnp.where(sk == 8, one, zero)
        + jnp.where(sk == 7, one * jnp.maximum(live, right["gz"]), zero)
        + jnp.where(sk == 15, one * right["gz"], zero)
    )
    for y in range(16):
        mult_y = {0: left["gy"], 7: 1.0, 8: 1.0, 15: right["gy"]}.get(y, 0.0)
        inv_yz[y] = 1.0 / (mult_z * (1.0 + mult_y))

    def plane(t, side):
        return 15 - t if side else t

    def inv_x(t, side):
        outer = right["gx"] if side else left["gx"]
        return 1.0 - 0.5 * (flag(t == 0) * outer + flag(t == 7))

    def turn(w):
        return w.astype(F32).T.astype(BF16)

    def half(w):
        return (w.astype(F32) * 0.5).astype(BF16)

    for l in range(2):
        w_first[l] = half(jnp.concatenate([edge_w[l, 0], node_in[l, :H]], 1))
        w_agg[l] = half(node_in[l, H:])
        w_out_t[l] = half(turn(node_out[l]))
        w_in_t[l] = jnp.concatenate([turn(node_in[l, :H]), turn(node_in[l, H:])], 1)
        two_t = half(turn(edge_w[l, 1]))
        w_two_t[l] = jnp.concatenate([two_t, two_t], 0)
        w_one_t[l] = turn(edge_w[l, 0])
    half_bias[...] = biases[...] * 0.5
    for u in units:
        u[0][...] = jnp.zeros_like(u[0])
    bias_acc[...] = jnp.zeros_like(bias_acc)

    at_one = ((2, 0), (0, 0))
    at_two = ((1, 0), (0, 128))
    at_in = ((1, 128), (0, 256))
    at_out = ((1, 384), (0, 512))
    at_bias = (((2, 128), (1, 512)), ((0, 640), (0, 641)))

    def add_grad(place, shift, value):
        u, row = place
        units[u][0][row + shift : row + shift + value.shape[0]] += value

    def steps(order, body, before=None, after=None):
        before, after = before or {}, after or {}

        def step(i, _):
            for k, todo in before.items():
                pl.when(i == k)(todo)
            body(order(i))
            for k, todo in after.items():
                pl.when(i == k)(todo)
            return 0

        lax.fori_loop(0, 8, step, 0)

    def ascending(i):
        return i

    def first_last(i):
        return lax.rem(i + 1, 8)

    def first_middle(i):
        late = lax.div(i, 4)
        return (1 - late) * (i + 1) + late * i * lax.div(i + 3, 8)

    def roll_up(x):
        return pltpu.roll(x.reshape(16, 8, H), 7, 1).reshape(8, 16, H)

    def roll_down(x):
        return pltpu.roll(x.reshape(16, 8, H), 1, 1).reshape(8, 16, H)

    def spread_y(u):
        pad = jnp.zeros((1, 16, H), F32)
        return jnp.concatenate([pad, u], 0) - jnp.concatenate([u, pad], 0)

    def put_first(l, p, h_plane):
        both = mm(h_plane, w_first[l])
        pre_a[p] = both[:, :H].reshape(16, 16, H)
        pre_n[p] = both[:, H:].reshape(16, 16, H)

    def put_field(p, r):
        r = r.reshape(16, 16, H) * row_live
        low, high = r[:, :8], r[:, 8:]
        k = lax.broadcasted_iota(jnp.int32, (16, 8, H), 1)
        none = jnp.zeros((16, 8, H), F32)
        low2 = low + jnp.where(k == 7, pltpu.roll(high, 7, 1), none)
        high2 = high + jnp.where(k == 0, pltpu.roll(low, 1, 1), none)
        r = jnp.concatenate([low2, high2], 1)
        joint = r[7:8] + r[8:9]
        field[p] = jnp.concatenate([r[:7], joint, joint, r[9:]], 0)

    def remote(src, dst, sem, n, to):
        send, recv = sem
        return pltpu.make_async_remote_copy(
            src_ref=src,
            dst_ref=dst,
            send_sem=send.at[n],
            recv_sem=recv.at[n],
            device_id=to,
            device_id_type=MESH,
        )

    def start(copies):
        for c in copies:
            c.start()

    def wait(copies):
        for c in copies:
            c.wait()

    def x_copies(e):
        sem = (ex_send.at[e], ex_recv.at[e])
        return [
            remote(field.at[0], x_in.at[e, 1], sem, 0, device(gx=-1)),
            remote(field.at[15], x_in.at[e, 0], sem, 1, device(gx=1)),
        ]

    def group_copies(e, g):
        sem = (ex_send.at[e], ex_recv.at[e])
        at = pl.ds(2 * GROUPS[g][0], 2 * (GROUPS[g][1] - GROUPS[g][0]))
        n = 2 + 8 * g
        copies = []
        for f in (0, 1):
            move = 2 * f - 1
            copies.append(
                remote(y_out.at[e, f, at], y_in.at[e, 1 - f, at], sem, n + f, device(gy=move))
            )
            copies.append(
                remote(z_out.at[e, f, at], z_in.at[e, 1 - f, at], sem, n + 2 + f, device(gz=move))
            )
            for fy in (0, 1):
                copies.append(
                    remote(
                        yz_out.at[e, g, f, fy],
                        yz_in.at[e, g, 1 - f, 1 - fy],
                        sem,
                        n + 4 + 2 * f + fy,
                        device(gy=2 * fy - 1, gz=move),
                    )
                )
        return copies

    def line(t, side):
        g = lax.div(t + 3, 4)
        return g, 2 * (t + 3 - 4 * g) + side

    def pack(e, t):
        for side in (0, 1):
            p, s = plane(t, side), 2 * t + side
            g, row = line(t, side)
            y_out[e, 0, s] = field[p, 0]
            y_out[e, 1, s] = field[p, 15]
            for f in (0, 1):
                if f:
                    z = field[p, :, 7, :] * (1.0 - live) + field[p, :, 15, :] * live
                else:
                    z = field[p, :, 0, :]
                z_out[e, f, s] = z
                yz_out[e, g, f, 0, pl.ds(row, 1), :] = z[0:1]
                yz_out[e, g, f, 1, pl.ds(row, 1), :] = z[15:16]

    def send_x(e):
        return lambda: start(x_copies(e))

    def send(e, g):
        return lambda: start(group_copies(e, g))

    def take(e, g):
        return lambda: wait(group_copies(e, g))

    def join_middle(e):
        joint = field[7] + field[8]
        field[7] = joint
        field[8] = joint
        pack(e, 7)

    def take_x(e):
        wait(x_copies(e))
        field[0] = field[0] + x_in[e, 0] * left["gx"]
        field[15] = field[15] + x_in[e, 1] * right["gx"]
        pack(e, 0)

    def summed(e, t, side):
        p, s = plane(t, side), 2 * t + side
        g, row = line(t, side)
        z = []
        for f in (0, 1):
            z.append(
                z_in[e, f, s]
                + yz_in[e, g, f, 0, pl.ds(row, 1), :] * first_y
                + yz_in[e, g, f, 1, pl.ds(row, 1), :] * last_y
            )
        whole = field[p]
        whole = jnp.concatenate(
            [
                whole[0:1] + (y_in[e, 0, s] * left["gy"])[None],
                whole[1:15],
                whole[15:16] + (y_in[e, 1, s] * right["gy"])[None],
            ],
            0,
        )
        return whole + z[0][:, None, :] * bottom_in + z[1][:, None, :] * top_in

    def messages(l, e):
        carry[...] = jnp.zeros_like(carry)
        bias = half_bias[l, 0:1]

        def body(t):
            inner = 1.0 - flag(t == 7)
            for side in (0, 1):
                p = plane(t, side)
                nxt = jnp.maximum(14 - t, 8) if side else jnp.minimum(t + 1, 7)
                for q in (0, 1):
                    ys = slice(8 * q, 8 * q + 8)
                    mine = pre_a[p, ys]
                    biased = mine - bias
                    if side:
                        ux, sx = act((mine + bias) - pre_a[nxt, ys])
                    else:
                        ux, sx = act(pre_a[nxt, ys] - biased)
                    ux = ux * inner
                    slope_x[l, p, ys] = sx * inner
                    total = ux - carry[side, ys] if side else carry[side, ys] - ux
                    carry[side, ys] = ux
                    uy, sy = act(mine[1:] - biased[:7])
                    slope_y[l, p, 8 * q : 8 * q + 7] = sy
                    total = total + spread_y(uy)
                    uz, sz = act(roll_up(mine) - biased)
                    uz = uz * not_top
                    slope_z[l, p, ys] = sz * not_top
                    total = total + roll_down(uz) - uz
                    spread[l, p, ys] = total.astype(BF16)
                put_field(p, mm(flat(spread[l, p]), edge_w[l, 1]))
            pack(e, t)

        steps(ascending, body, after={0: send_x(e), 4: send(e, 1)})
        join_middle(e)
        send(e, 2)()
        take_x(e)
        send(e, 0)()

    def node(l, e, t, side):
        p = plane(t, side)
        a = (summed(e, t, side) * (inv_yz[...] * inv_x(t, side))).astype(BF16)
        agg[l, p] = a
        pre = mm(flat(a), w_agg[l]) + flat(pre_n[p]) + half_bias[l, 1:2]
        v, slope = act(pre)
        v = v.astype(BF16)
        active[l, p] = v.reshape(16, 16, H)
        return v, slope

    def node_back(l, t, side, g, slope):
        p = plane(t, side)
        dpn = mm(g, w_out_t[l]) * slope
        bias_acc[l, 1] = bias_acc[l, 1] + jnp.sum(dpn.reshape(16, 16, H), 0)
        dpn = dpn.astype(BF16)
        g_now[p] = g.reshape(16, 16, H)
        d_now[p] = dpn.reshape(16, 16, H)
        dx = mm(dpn, w_in_t[l])
        dh[p] = (g.astype(F32) + dx[:, :H]).reshape(16, 16, H)
        put_field(p, dx[:, H:].reshape(16, 16, H) * (inv_yz[...] * inv_x(t, side)))

    def by_fours(body):
        def step(i, _):
            body(pl.ds(4 * i, 4))
            return 0

        lax.fori_loop(0, 4, step, 0)

    def node_grads(l, h_ref):
        def body(at):
            d = flat(d_now[at])
            add_grad(at_out[l], 0, mm_rows(flat(active[l, at]), flat(g_now[at])))
            add_grad(at_in[l], 0, mm_rows(flat(h_ref[at]), d))
            add_grad(at_in[l], H, mm_rows(flat(agg[l, at]), d))

        by_fours(body)

    def first_grad(l, h_ref):
        by_fours(lambda at: add_grad(at_one[l], 0, mm_rows(flat(h_ref[at]), flat(p_now[at]))))

    def edge_first(l, e, after=None):
        def body(t):
            for side in (0, 1):
                p = plane(t, side)
                dr = flat(summed(e, t, side) * row_live)
                hi = dr.astype(BF16)
                lo = (dr - hi.astype(F32)).astype(BF16)
                pair = jnp.concatenate([hi, lo], 1)
                pre_a[p] = mm(pair, w_two_t[l]).reshape(16, 16, H)
                both = mm_rows(flat(spread[l, p]), pair)
                add_grad(at_two[l], 0, both[:, :H] + both[:, H:])

        steps(
            first_last,
            body,
            before={0: take(e, 1), 4: take(e, 2), 7: take(e, 0)},
            after=after,
        )

    def edge_back(l, t, side):
        p = plane(t, side)
        nxt = jnp.maximum(14 - t, 8) if side else jnp.minimum(t + 1, 7)
        for q in (0, 1):
            ys = slice(8 * q, 8 * q + 8)
            mine = pre_a[p, ys]
            if side:
                dx = (mine - pre_a[nxt, ys]) * slope_x[l, p, ys]
                total = dx - carry[side, ys]
            else:
                dx = (pre_a[nxt, ys] - mine) * slope_x[l, p, ys]
                total = carry[side, ys] - dx
            carry[side, ys] = dx
            dy = (mine[1:] - mine[:7]) * slope_y[l, p, 8 * q : 8 * q + 7]
            total = total + spread_y(dy)
            dz = (roll_up(mine) - mine) * slope_z[l, p, ys]
            total = total + roll_down(dz) - dz
            bias_acc[l, 0] = bias_acc[l, 0] + (
                jnp.sum(dx, 0) + jnp.sum(dy, 0) + jnp.sum(dz, 0)
            )
            p_now[p, ys] = total.astype(BF16)
        return (flat(dh[p]) + mm(flat(p_now[p]), w_one_t[l])).astype(BF16)

    def stage_copies(u, stage):
        (buf, red_y, sum_y, red_x, sum_x, red_z, sum_z, gat_x, gat_y, send_sem, recv_sem) = units[u]
        sem = (send_sem, recv_sem)
        part_y, part_x = UNITS[u] // n_y, UNITS[u] // n_y // n_x

        def part(index, rows):
            return pl.ds(pl.multiple_of(index * rows, 8), rows)

        if stage == 0:
            return [
                remote(buf.at[part(peer("gy", d), part_y)], red_y.at[d - 1], sem, d - 1, device(gy=d))
                for d in range(1, n_y)
            ]
        n = n_y - 2
        if stage == 1:
            return [
                remote(sum_y.at[part(peer("gx", d), part_x)], red_x.at[d - 1], sem, n + d, device(gx=d))
                for d in range(1, n_x)
            ]
        n += n_x - 1
        if stage == 2:
            return [
                remote(sum_x, red_z.at[i_z], sem, n + d, device(gz=d)) for d in range(1, n_z)
            ]
        n += n_z - 1
        if stage == 3:
            return [
                remote(sum_z, gat_x.at[part(i_x, part_x)], sem, n + d, device(gx=d))
                for d in range(1, n_x)
            ]
        n += n_x - 1
        return [
            remote(gat_x, gat_y.at[part(i_y, part_y)], sem, n + d, device(gy=d))
            for d in range(1, n_y)
        ]

    def reduce_step(u, stage):
        (buf, red_y, sum_y, red_x, sum_x, red_z, sum_z, gat_x, gat_y, _, _) = units[u]
        part_y, part_x = UNITS[u] // n_y, UNITS[u] // n_y // n_x
        mine_y = pl.ds(pl.multiple_of(i_y * part_y, 8), part_y)
        mine_x = pl.ds(pl.multiple_of(i_x * part_x, 8), part_x)

        def run():
            if stage > 0:
                wait(stage_copies(u, stage - 1))
            if stage == 1:
                total = buf[mine_y]
                for d in range(1, n_y):
                    total = total + red_y[d - 1]
                sum_y[...] = total
            if stage == 2:
                total = sum_y[mine_x]
                for d in range(1, n_x):
                    total = total + red_x[d - 1]
                sum_x[...] = total
                red_z[i_z] = total
            if stage == 3:
                total = red_z[0]
                for d in range(1, n_z):
                    total = total + red_z[d]
                total = total * scale
                sum_z[...] = total
                gat_x[mine_x] = total
            if stage == 4:
                gat_y[mine_y] = gat_x[...]
            if stage < 5:
                start(stage_copies(u, stage))

        return run

    def put_out(place, rows):
        u, row = place
        return units[u][8][row : row + rows]

    def finish_bias(l, kind):
        u, row = at_bias[l][kind]
        units[u][0][row : row + 1] = jnp.sum(bias_acc[l, kind], 0, keepdims=True)

    def first(t):
        for side in (0, 1):
            p = plane(t, side)
            put_first(0, p, flat(state[p]))

    steps(ascending, first)
    messages(0, 0)

    def middle(t):
        for side in (0, 1):
            p = plane(t, side)
            v, slope = node(0, 0, t, side)
            slope_n[p] = slope.reshape(16, 16, H)
            nxt = (flat(state[p]).astype(F32) + mm(v, node_out[0])).astype(BF16)
            h_one[p] = nxt.reshape(16, 16, H)
            put_first(1, p, nxt)

    steps(first_last, middle, before={0: take(0, 1), 4: take(0, 2), 7: take(0, 0)})
    messages(1, 1)

    def last(t):
        for side in (0, 1):
            p = plane(t, side)
            v, slope = node(1, 1, t, side)
            g = flat((cotangent[p].astype(F32) * row_live).astype(BF16))
            node_back(1, t, side, g, slope)
        pack(2, t)

    def after_outer():
        start(x_copies(2))
        start(group_copies(2, 1))

    steps(
        first_middle,
        last,
        before={0: take(1, 1), 4: take(1, 0), 5: take(1, 2)},
        after={4: after_outer},
    )
    join_middle(2)
    send(2, 2)()
    take_x(2)
    send(2, 0)()
    node_grads(1, h_one)
    edge_first(1, 2)
    carry[...] = jnp.zeros_like(carry)

    def turnover(t):
        for side in (0, 1):
            g = edge_back(1, t, side)
            node_back(0, t, side, g, flat(slope_n[plane(t, side)]))
        pack(3, t)

    steps(ascending, turnover, after={0: send_x(3), 4: send(3, 1)})
    join_middle(3)
    send(3, 2)()
    take_x(3)
    send(3, 0)()
    first_grad(1, h_one)
    finish_bias(1, 0)
    finish_bias(1, 1)
    reduce_step(0, 0)()
    node_grads(0, state)
    finish_bias(0, 1)
    edge_first(0, 3, after={1: reduce_step(0, 1)})
    reduce_step(1, 0)()
    reduce_step(0, 2)()
    carry[...] = jnp.zeros_like(carry)

    def final(t):
        for side in (0, 1):
            p = plane(t, side)
            g = edge_back(0, t, side)
            state_grad[p] = g.reshape(16, 16, H)
            add_grad(at_one[0], 0, mm_rows(flat(state[p]), flat(p_now[p])))

    steps(
        ascending,
        final,
        after={2: reduce_step(1, 1), 4: reduce_step(0, 3), 7: reduce_step(1, 2)},
    )
    finish_bias(0, 0)
    reduce_step(2, 0)()
    reduce_step(0, 4)()
    reduce_step(2, 1)()
    reduce_step(1, 3)()
    reduce_step(2, 2)()
    reduce_step(1, 4)()
    reduce_step(2, 3)()
    reduce_step(0, 5)()
    reduce_step(1, 5)()
    for l in range(2):
        edge_grads[l, 1] = put_out(at_two[l], H)
        node_in_grad[l] = put_out(at_in[l], 2 * H)
        node_out_grad[l] = put_out(at_out[l], H)
    reduce_step(2, 4)()
    reduce_step(2, 5)()
    for l in range(2):
        edge_grads[l, 0] = put_out(at_one[l], H)
        for kind in (0, 1):
            bias_grads[l, kind : kind + 1] = put_out(at_bias[l][kind], 1)


def on_device(sizes, state, cotangent, counts, edge_weights, node_in, node_out, biases):
    n_x, n_y, n_z = sizes
    shape = state.shape
    nodes = (shape[0] * n_x) * (shape[1] * n_y) * (3 * shape[2] * n_z // 4) * shape[3]
    planes = (shape[0], shape[1], shape[2] * shape[3], H)
    vmem = pl.BlockSpec(memory_space=pltpu.VMEM)
    scratch = [
        pltpu.VMEM((2, H, 2 * H), BF16),
        pltpu.VMEM((2, H, H), BF16),
        pltpu.VMEM((2, H, H), BF16),
        pltpu.VMEM((2, H, 2 * H), BF16),
        pltpu.VMEM((2, 2 * H, H), BF16),
        pltpu.VMEM((2, H, H), BF16),
        pltpu.VMEM((2, 2, H), F32),
    ]
    scratch += [pltpu.VMEM(planes, BF16)] * 4
    scratch += [pltpu.VMEM(planes, F32)] * 4
    scratch += [pltpu.VMEM((2,) + planes, F32)] * 3
    scratch += [pltpu.VMEM(planes, F32)]
    scratch += [pltpu.VMEM((2,) + planes, BF16)] * 3
    scratch += [
        pltpu.VMEM(planes[1:], F32),
        pltpu.VMEM((2,) + planes[1:], F32),
        pltpu.VMEM((2, 2, 16, H), F32),
    ]
    scratch += [pltpu.VMEM((4, 2) + planes[1:], F32)]
    scratch += [pltpu.VMEM((4, 2, 16, 16, H), F32)] * 4
    scratch += [pltpu.VMEM((4, 3, 2, 2, 8, H), F32)] * 2
    scratch += [pltpu.SemaphoreType.DMA((4, 26))] * 2
    n_stage = 2 * (n_x - 1) + 2 * (n_y - 1) + n_z - 1
    for rows in UNITS:
        part_y, part_x = rows // n_y, rows // n_y // n_x
        scratch += [
            pltpu.VMEM((rows, H), F32),
            pltpu.VMEM((n_y - 1, part_y, H), F32),
            pltpu.VMEM((part_y, H), F32),
            pltpu.VMEM((n_x - 1, part_x, H), F32),
            pltpu.VMEM((part_x, H), F32),
            pltpu.VMEM((n_z, part_x, H), F32),
            pltpu.VMEM((part_x, H), F32),
            pltpu.VMEM((part_y, H), F32),
            pltpu.VMEM((rows, H), F32),
        ]
        scratch += [pltpu.SemaphoreType.DMA((n_stage,))] * 2
    outs = pl.pallas_call(
        functools.partial(kernel, sizes, 1.0 / math.sqrt(nodes)),
        out_shape=(
            jax.ShapeDtypeStruct(planes, BF16),
            jax.ShapeDtypeStruct((2, 2, H, H), F32),
            jax.ShapeDtypeStruct((2, 2 * H, H), F32),
            jax.ShapeDtypeStruct((2, H, H), F32),
            jax.ShapeDtypeStruct((2, 2, H), F32),
        ),
        in_specs=[vmem, vmem, pl.BlockSpec(memory_space=pltpu.SMEM), vmem, vmem, vmem, vmem],
        out_specs=(vmem,) * 5,
        scratch_shapes=scratch,
        compiler_params=pltpu.CompilerParams(
            collective_id=0, has_side_effects=True, vmem_limit_bytes=66_000_000
        ),
        name="layers",
    )(
        state.reshape(planes),
        cotangent.reshape(planes),
        counts,
        edge_weights,
        node_in,
        node_out,
        biases,
    )
    return (outs[0].reshape(shape),) + tuple(outs[1:])


def solution(mesh):
    sizes = tuple(mesh.shape[name] for name in AXES)
    grid = P("gx", "gy", "gz", None, None)
    return jax.shard_map(
        functools.partial(on_device, sizes),
        mesh=mesh,
        in_specs=(grid, grid, P("gz"), P(), P(), P(), P()),
        out_specs=(grid, P(), P(), P(), P()),
        check_vma=False,
    )
```

time: 161 us -> 114 us (0.71)
  Pallas kernels: 154 us -> 107 us
    pallas_call x1, Pallas kernels: 154 us -> 107 us  [on_device(): pl.pallas_call(functools.partial(kernel, sizes, 1.0 / math.sqrt(nodes)),...]
where the time goes in v2:
time: 114 us
  Pallas kernels  107 us (94%)
  local copies, waits for them, and re-layouts  5.75 us (5%)
  between operations  1.3 us (1%)
    pallas_call x1, Pallas kernels, on_device(): pl.pallas_call(functools.partial(kernel, sizes, 1.0 / math.sqrt(nodes)),...  107 us
    unnamed x13, local copies, waits for them, and re-layouts  5.75 us

profile of v2, /device:TPU:1, one launch (start us, length us, event | category | flops | bytes accessed | tf_op | source)
XLA Modules:
  0.0 113.6 jit_solution(1000141893034775224)
XLA Ops:
  1.3 106.5 %layers.1 = (bf16[16,16,16,128]{3,2,1,0:T(8,128)(2,1)}, f32[2,2,128,128]{3,2,1,0:T(8,128)}, f32[2,256,128]{2,1,0:T(8,128)}, f32[2,128,128]{2,1,0:T(8,128)}, f32[2,2,128]{2,1,0:T(2,128)}) custom-call(bf16[16,16,16,128]{3,2,1,0:T(8,128)(2,1)} %bitcast.3, bf16[16,16,16,128]{3,2,1,0:T(8,128)(2,1)} %bitcast.4, s32[1]{0:T(128)S(6)} %copy.17.refs_2_, ...), custom_call_target="tpu_custom_call" | custom-call | tf_op jit(solution)/shard_map/layers/pallas_call | solution.py:636
  107.8 0.0 copy-start.1
  107.8 2.5 %copy.18 = bf16[16,16,2,8,128]{4,3,2,1,0:T(8,128)(2,1)} copy(bf16[16,16,2,8,128]{4,3,2,1,0:T(8,128)(2,1)} %bitcast.5) | data formatting | bytes 2097152
  110.3 0.0 copy-done.1
  110.3 0.0 copy-start
  110.3 0.7 copy.19
  111.0 0.3 copy-done
  111.3 0.0 copy-start.2
  111.3 0.7 copy.20
  112.0 0.3 copy-done.2
  112.3 0.0 copy-start.3
  112.3 0.7 copy.21
  113.0 0.0 copy-done.3
  113.0 0.6 copy.22
Async XLA Ops:
  107.8 2.5 %copy-start.1 = (f32[2,2,128,128]{3,2,1,0:T(8,128)S(1)}, f32[2,2,128,128]{3,2,1,0:T(8,128)}, u32[]{:S(2)}) copy-start(f32[2,2,128,128]{3,2,1,0:T(8,128)} %get-tuple-element.21) | copy-start | bytes 786436
  110.3 1.0 copy-start
  111.3 1.0 copy-start.2
  112.3 0.7 copy-start.3

commit v3 on v2

v3 whole, which is shorter than its diff:
```python
import functools
import math

import jax
import jax.numpy as jnp
from jax import lax
from jax.experimental import pallas as pl
from jax.experimental.pallas import tpu as pltpu
from jax.sharding import PartitionSpec as P

F32 = jnp.float32
BF16 = jnp.bfloat16
H = 128
MESH = pl.DeviceIdType.MESH
AXES = ("gx", "gy", "gz")
UNITS = (512, 512, 256, 256)
GROUPS = ((0, 1), (1, 3), (3, 5), (5, 7), (7, 8))
SIDES = (0, 1)
STARTS = (0, 4, 8, 12)


def mm(a, b):
    return jnp.dot(a, b, preferred_element_type=F32)


def mm_rows(a, b):
    return lax.dot_general(a, b, (((0,), (0,)), ((), ())), preferred_element_type=F32)


def act(x):
    t = jnp.tanh(x)
    m = x * t
    return x + m, (1.0 + t) * ((1.0 + x) - m)


def flat(x):
    return x.reshape(-1, x.shape[-1])


def kernel(sizes, scale, *refs):
    (
        state, cotangent_hbm, counts, edge_w, node_in, node_out, biases,
        state_grad_hbm, grads,
        cotangent, state_grad, load_sem,
        w_first, w_agg, w_out_t, w_in_t, w_two_t, w_one_t, half_bias,
        h_one, g_now, d_now, p_now, pre_a, pre_n, field, dh,
        slope_x, slope_y, slope_z, slope_n, spread, agg, active, inv_yz, carry, bias_acc,
        x_in, rim_out, rim_in, ex_send, ex_recv,
    ) = refs[:42]
    units = [refs[42 + 11 * u : 53 + 11 * u] for u in range(len(UNITS))]
    n_x, n_y, n_z = sizes
    i_x, i_y, i_z = (lax.axis_index(name) for name in AXES)
    here = dict(zip(AXES, (i_x, i_y, i_z)))
    size = dict(zip(AXES, sizes))

    def peer(axis, d):
        return lax.rem(here[axis] + d, size[axis])

    def device(**moves):
        return tuple(peer(a, moves[a] % size[a]) if a in moves else here[a] for a in AXES)

    barrier = pltpu.get_barrier_semaphore()
    partners = [device(**{a: d}) for a in AXES for d in range(1, size[a])]
    partners += [device(gy=dy, gz=dz) for dy in (-1, 1) for dz in (-1, 1)]
    for q in partners:
        pl.semaphore_signal(barrier, inc=1, device_id=q, device_id_type=MESH)
    load = pltpu.make_async_copy(cotangent_hbm, cotangent, load_sem.at[0])
    load.start()

    def flag(cond):
        return jnp.where(cond, 1.0, 0.0).astype(F32)

    live = flag(counts[0] > 1)
    left = {a: flag(here[a] > 0) for a in AXES}
    right = {a: flag(here[a] < size[a] - 1) for a in AXES}

    sk = lax.broadcasted_iota(jnp.int32, (16, H), 0)
    one = jnp.ones((16, H), F32)
    zero = jnp.zeros((16, H), F32)
    row_live = jnp.where(sk < 8, one, one * live)
    not_top = jnp.where((sk == 7) | (sk == 15), zero, one)
    bottom = jnp.where(sk == 0, one, zero)
    top = jnp.where(sk == 7, one * (1.0 - live), jnp.where(sk == 15, one * live, zero))
    bottom_in = bottom * left["gz"]
    top_in = top * right["gz"]
    first_y = bottom * left["gy"]
    last_y = jnp.where(sk == 15, one * right["gy"], zero)
    mult_z = (
        one
        + jnp.where(sk == 0, one * left["gz"], zero)
        + jnp.where(sk == 8, one, zero)
        + jnp.where(sk == 7, one * jnp.maximum(live, right["gz"]), zero)
        + jnp.where(sk == 15, one * right["gz"], zero)
    )
    for y in range(16):
        mult_y = {0: left["gy"], 7: 1.0, 8: 1.0, 15: right["gy"]}.get(y, 0.0)
        inv_yz[y] = 1.0 / (mult_z * (1.0 + mult_y))

    def plane(t, side):
        return 15 - t if side else t

    def inv_x(t, side):
        outer = right["gx"] if side else left["gx"]
        return 1.0 - 0.5 * (flag(t == 0) * outer + flag(t == 7))

    def turn(w):
        return w.astype(F32).T.astype(BF16)

    def half(w):
        return (w.astype(F32) * 0.5).astype(BF16)

    for l in range(2):
        w_first[l] = half(jnp.concatenate([edge_w[l, 0], node_in[l, :H]], 1))
        w_agg[l] = half(node_in[l, H:])
        w_out_t[l] = half(turn(node_out[l]))
        w_in_t[l] = jnp.concatenate([turn(node_in[l, :H]), turn(node_in[l, H:])], 1)
        two_t = half(turn(edge_w[l, 1]))
        w_two_t[l] = jnp.concatenate([two_t, two_t], 0)
        w_one_t[l] = turn(edge_w[l, 0])
    half_bias[...] = biases[...] * 0.5
    for u in units:
        u[0][...] = jnp.zeros_like(u[0])
    bias_acc[...] = jnp.zeros_like(bias_acc)

    at_one = ((3, 0), (1, 0))
    at_two = ((2, 0), (0, 384))
    at_in = ((1, 128), (0, 0))
    at_out = ((1, 384), (0, 256))
    at_bias = (((3, 128), (2, 128)), ((2, 129), (2, 130)))

    def add_grad(place, shift, value):
        u, row = place
        units[u][0][row + shift : row + shift + value.shape[0]] += value

    def steps(order, body, before=None, after=None):
        before, after = before or {}, after or {}

        def step(i, _):
            for k, todo in before.items():
                pl.when(i == k)(todo)
            body(order(i))
            for k, todo in after.items():
                pl.when(i == k)(todo)
            return 0

        lax.fori_loop(0, 8, step, 0)

    def ascending(i):
        return i

    def first_late(i):
        late = lax.div(i, 6)
        return (1 - late) * (i + 1) + late * 7 * (i - 6)

    def first_third(i):
        late = lax.div(i + 5, 8)
        return (1 - late) * lax.rem(i + 1, 3) + late * i

    def roll_k(x, shift):
        n = x.shape[0]
        return pltpu.roll(x.reshape(2 * n, 8, H), shift, 1).reshape(n, 16, H)

    def rows(side, y0):
        return slice(256 * side + 16 * y0, 256 * side + 16 * y0 + 64)

    def cube(x):
        return x.reshape(-1, 16, H)

    def put_first(l, t, h_rows):
        both = mm(h_rows, w_first[l])
        for side in SIDES:
            p = plane(t, side)
            pre_a[p] = cube(both[256 * side : 256 * side + 256, :H])
            pre_n[p] = cube(both[256 * side : 256 * side + 256, H:])

    def put_field(t, chunk):
        k = lax.broadcasted_iota(jnp.int32, (4, 8, H), 1)
        none = jnp.zeros((4, 8, H), F32)
        for side in SIDES:
            p = plane(t, side)
            for y0 in STARTS:
                r = chunk(side, y0)
                low, high = r[:, :8], r[:, 8:] * live
                low2 = low + jnp.where(k == 7, pltpu.roll(high, 7, 1), none)
                high2 = high + jnp.where(k == 0, pltpu.roll(low, 1, 1), none)
                r = jnp.concatenate([low2, high2], 1)
                if y0 == 4:
                    held = r[3:4]
                    field[p, 4:7] = r[:3]
                elif y0 == 8:
                    joint = held + r[0:1]
                    field[p, 7:9] = jnp.concatenate([joint, joint], 0)
                    field[p, 9:12] = r[1:]
                else:
                    field[p, y0 : y0 + 4] = r

    def edge_chunks(t, side, per_edge):
        p = plane(t, side)
        nxt = jnp.maximum(14 - t, 8) if side else jnp.minimum(t + 1, 7)
        zero_row = jnp.zeros((1, 16, H), F32)
        out = []
        for y0 in STARTS:
            ys = slice(y0, y0 + 4)
            mine = pre_a[p, ys]
            if side:
                ux = per_edge(0, pre_a[nxt, ys], mine, p, y0, 4)
                total = ux - carry[side, ys]
            else:
                ux = per_edge(0, mine, pre_a[nxt, ys], p, y0, 4)
                total = carry[side, ys] - ux
            carry[side, ys] = ux
            n = 3 if y0 % 8 else 4
            uy = per_edge(1, mine[:n], pre_a[p, y0 + 1 : y0 + 1 + n], p, y0, n)
            arriving = jnp.concatenate([held if y0 % 8 else zero_row, uy[:3]], 0)
            held = uy[3:4] if n == 4 else None
            leaving = uy if n == 4 else jnp.concatenate([uy, zero_row], 0)
            total = total + (arriving - leaving)
            uz = per_edge(2, mine, roll_k(mine, 7), p, y0, 4)
            total = total + (roll_k(uz, 1) - uz)
            out.append(total.astype(BF16))
        return out

    def remote(src, dst, sem, n, to):
        send, recv = sem
        return pltpu.make_async_remote_copy(
            src_ref=src,
            dst_ref=dst,
            send_sem=send.at[n],
            recv_sem=recv.at[n],
            device_id=to,
            device_id_type=MESH,
        )

    def start(copies):
        for c in copies:
            c.start()

    def wait(src, dst, sem, n):
        whole = remote(src, dst, sem, n, device(gx=1))
        whole.wait_send()
        whole.wait_recv()

    def x_copies(e):
        sem = (ex_send.at[e], ex_recv.at[e])
        n = len(GROUPS)
        return [
            remote(field.at[0], x_in.at[e, 1], sem, n, device(gx=-1)),
            remote(field.at[15], x_in.at[e, 0], sem, n, device(gx=1)),
        ]

    def wait_x(e):
        wait(field.at[pl.ds(0, 2)], x_in.at[e], (ex_send.at[e], ex_recv.at[e]), len(GROUPS))

    def group_copies(e, g):
        sem = (ex_send.at[e], ex_recv.at[e])
        first = 32 if g == 0 else 0
        n = 32 * (GROUPS[g][1] - GROUPS[g][0])

        def one_copy(src, dst, count, to):
            return remote(
                rim_out.at[e, g, pl.ds(src, count)], rim_in.at[e, g, pl.ds(dst, count)], sem, g, to
            )

        copies = []
        for f in (0, 1):
            move = 2 * f - 1
            src, dst = 64 * f + first, 64 * (1 - f) + first
            copies.append(one_copy(src, dst, n, device(gy=move)))
            copies.append(one_copy(128 + src, 128 + dst, n, device(gz=move)))
            for fy in (0, 1):
                src, dst = 256 + 8 * (2 * f + fy), 256 + 8 * (3 - 2 * f - fy)
                copies.append(one_copy(src, dst, 8, device(gy=2 * fy - 1, gz=move)))
        return copies

    def wait_group(e, g):
        n = pl.ds(0, 128 * (GROUPS[g][1] - GROUPS[g][0]) + 32)
        wait(rim_out.at[e, g, n], rim_in.at[e, g, n], (ex_send.at[e], ex_recv.at[e]), g)

    def line(t, side):
        g = lax.div(t + 1, 2)
        return g, 2 * (t + 1 - 2 * g) + side

    def face(kind, f, row):
        return pl.ds(pl.multiple_of(128 * kind + 64 * f + 16 * row, 16), 16)

    def edge_line(f, fy, row):
        return pl.ds(256 + 8 * (2 * f + fy) + row, 1)

    def pack(e, t):
        for side in SIDES:
            p = plane(t, side)
            g, row = line(t, side)
            rim_out[e, g, face(0, 0, row)] = field[p, 0]
            rim_out[e, g, face(0, 1, row)] = field[p, 15]
            for f in (0, 1):
                if f:
                    z = field[p, :, 7, :] * (1.0 - live) + field[p, :, 15, :] * live
                else:
                    z = field[p, :, 0, :]
                rim_out[e, g, face(1, f, row)] = z
                rim_out[e, g, edge_line(f, 0, row)] = z[0:1]
                rim_out[e, g, edge_line(f, 1, row)] = z[15:16]

    def many(*todo):
        def run():
            for one_todo in todo:
                one_todo()

        return run

    def send_x(e):
        return lambda: start(x_copies(e))

    def send(e, g):
        return lambda: start(group_copies(e, g))

    def take(e, g):
        return lambda: wait_group(e, g)

    def outer(e):
        def run():
            wait_x(e)
            field[0] = field[0] + x_in[e, 0] * left["gx"]
            field[15] = field[15] + x_in[e, 1] * right["gx"]
            pack(e, 0)
            start(group_copies(e, 0))

        return run

    def join_middle(e):
        joint = field[7] + field[8]
        field[7] = joint
        field[8] = joint
        pack(e, 7)
        start(group_copies(e, 4))

    def sends(e):
        return {0: send_x(e), 2: send(e, 1), 4: send(e, 2), 6: many(send(e, 3), outer(e))}

    def takes(e):
        return {0: take(e, 1), 2: take(e, 2), 4: take(e, 3), 6: take(e, 0), 7: take(e, 4)}

    def summed(e, t, side):
        p = plane(t, side)
        g, row = line(t, side)
        z = []
        for f in (0, 1):
            z.append(
                rim_in[e, g, face(1, f, row)]
                + rim_in[e, g, edge_line(f, 0, row)] * first_y
                + rim_in[e, g, edge_line(f, 1, row)] * last_y
            )
        out = []
        for y0 in STARTS:
            r = field[p, y0 : y0 + 4]
            if y0 == 0:
                r = jnp.concatenate([r[0:1] + (rim_in[e, g, face(0, 0, row)] * left["gy"])[None], r[1:]], 0)
            if y0 == 12:
                r = jnp.concatenate([r[:3], r[3:4] + (rim_in[e, g, face(0, 1, row)] * right["gy"])[None]], 0)
            r = r + z[0][y0 : y0 + 4][:, None, :] * bottom_in
            out.append(r + z[1][y0 : y0 + 4][:, None, :] * top_in)
        return out

    def messages(l, e):
        carry[...] = jnp.zeros_like(carry)
        bias = half_bias[l, 0:1]
        slopes = (slope_x, slope_y, slope_z)

        def body(t):
            inner = 1.0 - flag(t == 7)

            def per_edge(dim, low, high, p, y0, n):
                u, slope = act((high - low) + bias)
                if dim == 0:
                    u, slope = u * inner, slope * inner
                if dim == 2:
                    u, slope = u * not_top, slope * not_top
                slopes[dim][l, p, y0 : y0 + n] = slope
                return u

            parts = []
            for side in SIDES:
                out = edge_chunks(t, side, per_edge)
                for y0, part in zip(STARTS, out):
                    spread[l, plane(t, side), y0 : y0 + 4] = part
                parts += [flat(part) for part in out]
            r = mm(jnp.concatenate(parts, 0), edge_w[l, 1])
            put_field(t, lambda side, y0: cube(r[rows(side, y0)]))
            pack(e, t)

        steps(ascending, body, after=sends(e))
        join_middle(e)

    def node(l, e, t):
        parts = []
        for side in SIDES:
            p = plane(t, side)
            inv = inv_x(t, side)
            for y0, part in zip(STARTS, summed(e, t, side)):
                a = (part * (inv_yz[y0 : y0 + 4] * inv)).astype(BF16)
                agg[l, p, y0 : y0 + 4] = a
                parts.append(flat(a))
        pre = mm(jnp.concatenate(parts, 0), w_agg[l])
        values, slopes = [], []
        for side in SIDES:
            p = plane(t, side)
            for y0 in STARTS:
                x = pre[rows(side, y0)] + flat(pre_n[p, y0 : y0 + 4]) + half_bias[l, 1:2]
                v, slope = act(x)
                v = v.astype(BF16)
                active[l, p, y0 : y0 + 4] = cube(v)
                values.append(v)
                slopes.append(slope)
        return jnp.concatenate(values, 0), slopes

    def node_back(l, t, g, slopes):
        dv = mm(g, w_out_t[l])
        total = jnp.zeros((16, H), F32)
        parts = []
        for i, slope in enumerate(slopes):
            d = dv[64 * i : 64 * i + 64] * slope
            total = total + jnp.sum(cube(d), 0)
            parts.append(d.astype(BF16))
        bias_acc[l, 1] = bias_acc[l, 1] + total
        d = jnp.concatenate(parts, 0)
        dx = mm(d, w_in_t[l])
        for side in SIDES:
            p = plane(t, side)
            g_now[p] = cube(g[256 * side : 256 * side + 256])
            d_now[p] = cube(d[256 * side : 256 * side + 256])
            for y0 in STARTS:
                at = rows(side, y0)
                dh[p, y0 : y0 + 4] = cube(g[at].astype(F32) + dx[at, :H])
        inv = [inv_x(t, side) for side in SIDES]
        put_field(
            t,
            lambda side, y0: cube(dx[rows(side, y0), H:])
            * (inv_yz[y0 : y0 + 4] * inv[side]),
        )

    def by_fours(body):
        def step(i, _):
            body(pl.ds(4 * i, 4))
            return 0

        lax.fori_loop(0, 4, step, 0)

    def node_grads(l, h_ref):
        def body(at):
            d = flat(d_now[at])
            add_grad(at_out[l], 0, mm_rows(flat(active[l, at]), flat(g_now[at])))
            add_grad(at_in[l], 0, mm_rows(flat(h_ref[at]), d))
            add_grad(at_in[l], H, mm_rows(flat(agg[l, at]), d))

        by_fours(body)

    def first_grad(l, h_ref):
        by_fours(lambda at: add_grad(at_one[l], 0, mm_rows(flat(h_ref[at]), flat(p_now[at]))))

    def edge_first(l, e, after=None):
        def body(t):
            pairs, spreads = [], []
            for side in SIDES:
                spreads.append(flat(spread[l, plane(t, side)]))
                for part in summed(e, t, side):
                    dr = flat(part * row_live)
                    hi = dr.astype(BF16)
                    lo = (dr - hi.astype(F32)).astype(BF16)
                    pairs.append(jnp.concatenate([hi, lo], 1))
            pair = jnp.concatenate(pairs, 0)
            r = mm(pair, w_two_t[l])
            for side in SIDES:
                pre_a[plane(t, side)] = cube(r[256 * side : 256 * side + 256])
            both = mm_rows(jnp.concatenate(spreads, 0), pair)
            add_grad(at_two[l], 0, both[:, :H] + both[:, H:])

        steps(first_late, body, before=takes(e), after=after)

    def edge_back(l, t):
        slopes = (slope_x, slope_y, slope_z)
        sums = []

        def per_edge(dim, low, high, p, y0, n):
            d = (high - low) * slopes[dim][l, p, y0 : y0 + n]
            sums.append(jnp.sum(d, 0))
            return d

        parts = []
        for side in SIDES:
            out = edge_chunks(t, side, per_edge)
            total = functools.reduce(jnp.add, sums)
            sums.clear()
            bias_acc[l, 0] = bias_acc[l, 0] + total
            for y0, part in zip(STARTS, out):
                p_now[plane(t, side), y0 : y0 + 4] = part
            parts += [flat(part) for part in out]
        back = jnp.concatenate(parts, 0)
        held = jnp.concatenate([flat(dh[plane(t, side)]) for side in SIDES], 0)
        return (held + mm(back, w_one_t[l])).astype(BF16), back

    def stage_copies(u, stage):
        (buf, red_y, sum_y, red_x, sum_x, red_z, sum_z, gat_x, gat_y, send_sem, recv_sem) = units[u]
        sem = (send_sem, recv_sem)
        part_y, part_x = UNITS[u] // n_y, UNITS[u] // n_y // n_x

        def part(index, rows):
            return pl.ds(pl.multiple_of(index * rows, 8), rows)

        if stage == 0:
            return [
                remote(buf.at[part(peer("gy", d), part_y)], red_y.at[d - 1], sem, 0, device(gy=d))
                for d in range(1, n_y)
            ]
        if stage == 1:
            return [
                remote(sum_y.at[part(peer("gx", d), part_x)], red_x.at[d - 1], sem, 1, device(gx=d))
                for d in range(1, n_x)
            ]
        if stage == 2:
            return [remote(sum_x, red_z.at[i_z], sem, 2, device(gz=d)) for d in range(1, n_z)]
        if stage == 3:
            return [
                remote(sum_z, gat_x.at[part(i_x, part_x)], sem, 3, device(gx=d))
                for d in range(1, n_x)
            ]
        return [
            remote(gat_x, gat_y.at[part(i_y, part_y)], sem, 4, device(gy=d))
            for d in range(1, n_y)
        ]

    def wait_stage(u, stage):
        (buf, red_y, sum_y, red_x, sum_x, red_z, sum_z, gat_x, gat_y, send_sem, recv_sem) = units[u]
        part_y, part_x = UNITS[u] // n_y, UNITS[u] // n_y // n_x
        most_y, most_x = pl.ds(0, UNITS[u] - part_y), pl.ds(0, part_y - part_x)
        most_z = pl.ds(0, n_z - 1)
        src, dst = (
            (buf.at[most_y], red_y),
            (sum_y.at[most_x], red_x),
            (red_z.at[most_z], red_z.at[most_z]),
            (gat_x.at[most_x], gat_x.at[most_x]),
            (gat_y.at[most_y], gat_y.at[most_y]),
        )[stage]
        wait(src, dst, (send_sem, recv_sem), stage)

    def reduce_step(u, stage):
        (buf, red_y, sum_y, red_x, sum_x, red_z, sum_z, gat_x, gat_y, _, _) = units[u]
        part_y, part_x = UNITS[u] // n_y, UNITS[u] // n_y // n_x
        mine_y = pl.ds(pl.multiple_of(i_y * part_y, 8), part_y)
        mine_x = pl.ds(pl.multiple_of(i_x * part_x, 8), part_x)

        def run():
            if stage > 0:
                wait_stage(u, stage - 1)
            if stage == 1:
                total = buf[mine_y]
                for d in range(1, n_y):
                    total = total + red_y[d - 1]
                sum_y[...] = total
            if stage == 2:
                total = sum_y[mine_x]
                for d in range(1, n_x):
                    total = total + red_x[d - 1]
                sum_x[...] = total
                red_z[i_z] = total
            if stage == 3:
                total = red_z[0]
                for d in range(1, n_z):
                    total = total + red_z[d]
                total = total * scale
                sum_z[...] = total
                gat_x[mine_x] = total
            if stage == 4:
                gat_y[mine_y] = gat_x[...]
            if stage < 5:
                start(stage_copies(u, stage))

        return run

    def finish_bias(l, kind):
        u, row = at_bias[l][kind]
        units[u][0][row : row + 1] = jnp.sum(bias_acc[l, kind], 0, keepdims=True)

    def two(ref, t):
        return jnp.concatenate([flat(ref[plane(t, side)]) for side in SIDES], 0)

    def put_two(ref, t, x):
        for side in SIDES:
            ref[plane(t, side)] = cube(x[256 * side : 256 * side + 256])

    steps(ascending, lambda t: put_first(0, t, two(state, t)))
    pl.semaphore_wait(barrier, len(partners))
    messages(0, 0)

    def middle(t):
        v, slopes = node(0, 0, t)
        put_two(slope_n, t, jnp.concatenate(slopes, 0))
        nxt = (two(state, t).astype(F32) + mm(v, node_out[0])).astype(BF16)
        put_two(h_one, t, nxt)
        put_first(1, t, nxt)

    steps(first_late, middle, before=takes(0))
    messages(1, 1)
    load.wait()

    def last(t):
        _, slopes = node(1, 1, t)
        g = two(cotangent, t)
        g = (cube(g).astype(F32) * row_live).astype(BF16)
        node_back(1, t, flat(g), slopes)
        pack(2, t)

    steps(
        first_third,
        last,
        before={0: take(1, 1), 2: take(1, 0), 3: take(1, 2), 5: take(1, 3), 7: take(1, 4)},
        after={1: send(2, 1), 2: send_x(2), 4: send(2, 2), 6: many(send(2, 3), outer(2))},
    )
    join_middle(2)
    node_grads(1, h_one)
    edge_first(1, 2)
    reduce_step(0, 0)()
    carry[...] = jnp.zeros_like(carry)

    def turnover(t):
        g, _ = edge_back(1, t)
        saved = [slope_n[plane(t, side), y0 : y0 + 4] for side in SIDES for y0 in STARTS]
        node_back(0, t, g, [flat(x) for x in saved])
        pack(3, t)

    after = sends(3)
    after[5] = reduce_step(0, 1)
    steps(ascending, turnover, after=after)
    join_middle(3)
    first_grad(1, h_one)
    node_grads(0, state)
    reduce_step(1, 0)()
    reduce_step(0, 2)()
    finish_bias(0, 1)
    finish_bias(1, 0)
    finish_bias(1, 1)
    edge_first(0, 3)
    reduce_step(2, 0)()
    reduce_step(1, 1)()
    reduce_step(0, 3)()
    carry[...] = jnp.zeros_like(carry)

    def final(t):
        g, back = edge_back(0, t)
        put_two(state_grad, t, g)
        add_grad(at_one[0], 0, mm_rows(two(state, t), back))

    steps(
        ascending,
        final,
        after={6: many(reduce_step(1, 2), reduce_step(0, 4), reduce_step(2, 1))},
    )
    finish_bias(0, 0)
    reduce_step(3, 0)()
    store = pltpu.make_async_copy(state_grad, state_grad_hbm, load_sem.at[1])
    store.start()
    reduce_step(3, 1)()
    reduce_step(1, 3)()
    reduce_step(2, 2)()
    reduce_step(3, 2)()
    reduce_step(0, 5)()
    reduce_step(1, 4)()
    reduce_step(2, 3)()
    reduce_step(3, 3)()
    reduce_step(1, 5)()
    reduce_step(2, 4)()
    reduce_step(2, 5)()
    row = 0
    for u in range(len(UNITS) - 1):
        grads[row : row + UNITS[u]] = units[u][8][...]
        row += UNITS[u]
    store.wait()
    reduce_step(3, 4)()
    reduce_step(3, 5)()
    grads[row : row + UNITS[3]] = units[3][8][...]


def write_out(state_in, grads, state_grad, edge_grads, node_in_grad, node_out_grad, bias_grads):
    state_grad[...] = state_in[...]
    edge_grads[0, 0] = grads[1280:1408]
    edge_grads[0, 1] = grads[1024:1152]
    edge_grads[1, 0] = grads[512:640]
    edge_grads[1, 1] = grads[384:512]
    node_in_grad[0] = grads[640:896]
    node_in_grad[1] = grads[0:256]
    node_out_grad[0] = grads[896:1024]
    node_out_grad[1] = grads[256:384]
    bias_grads[0, 0:1] = grads[1408:1409]
    bias_grads[0, 1:2] = grads[1152:1153]
    bias_grads[1, 0:1] = grads[1153:1154]
    bias_grads[1, 1:2] = grads[1154:1155]


def on_device(sizes, state, cotangent, counts, edge_weights, node_in, node_out, biases):
    n_x, n_y, n_z = sizes
    shape = state.shape
    nodes = (shape[0] * n_x) * (shape[1] * n_y) * (3 * shape[2] * n_z // 4) * shape[3]
    planes = (shape[0], shape[1], shape[2] * shape[3], H)
    vmem = pl.BlockSpec(memory_space=pltpu.VMEM)
    hbm = pl.BlockSpec(memory_space=pl.ANY)
    scratch = [
        pltpu.VMEM(planes, BF16),
        pltpu.VMEM(planes, BF16),
        pltpu.SemaphoreType.DMA((2,)),
        pltpu.VMEM((2, H, 2 * H), BF16),
        pltpu.VMEM((2, H, H), BF16),
        pltpu.VMEM((2, H, H), BF16),
        pltpu.VMEM((2, H, 2 * H), BF16),
        pltpu.VMEM((2, 2 * H, H), BF16),
        pltpu.VMEM((2, H, H), BF16),
        pltpu.VMEM((2, 2, H), F32),
    ]
    scratch += [pltpu.VMEM(planes, BF16)] * 4
    scratch += [pltpu.VMEM(planes, F32)] * 4
    scratch += [pltpu.VMEM((2,) + planes, F32)] * 3
    scratch += [pltpu.VMEM(planes, F32)]
    scratch += [pltpu.VMEM((2,) + planes, BF16)] * 3
    scratch += [
        pltpu.VMEM(planes[1:], F32),
        pltpu.VMEM((2,) + planes[1:], F32),
        pltpu.VMEM((2, 2, 16, H), F32),
    ]
    scratch += [pltpu.VMEM((4, 2) + planes[1:], F32)]
    scratch += [pltpu.VMEM((4, len(GROUPS), 288, H), F32)] * 2
    scratch += [pltpu.SemaphoreType.DMA((4, len(GROUPS) + 1))] * 2
    for rows in UNITS:
        part_y, part_x = rows // n_y, rows // n_y // n_x
        scratch += [
            pltpu.VMEM((rows, H), F32),
            pltpu.VMEM((n_y - 1, part_y, H), F32),
            pltpu.VMEM((part_y, H), F32),
            pltpu.VMEM((n_x - 1, part_x, H), F32),
            pltpu.VMEM((part_x, H), F32),
            pltpu.VMEM((n_z, part_x, H), F32),
            pltpu.VMEM((part_x, H), F32),
            pltpu.VMEM((part_y, H), F32),
            pltpu.VMEM((rows, H), F32),
        ]
        scratch += [pltpu.SemaphoreType.DMA((5,))] * 2
    outs = pl.pallas_call(
        functools.partial(kernel, sizes, 1.0 / math.sqrt(nodes)),
        out_shape=(
            jax.ShapeDtypeStruct(planes, BF16),
            jax.ShapeDtypeStruct((sum(UNITS), H), F32),
        ),
        in_specs=[vmem, hbm, pl.BlockSpec(memory_space=pltpu.SMEM), vmem, vmem, vmem, vmem],
        out_specs=(hbm, vmem),
        scratch_shapes=scratch,
        compiler_params=pltpu.CompilerParams(
            collective_id=0, has_side_effects=True, vmem_limit_bytes=66_000_000
        ),
        name="layers",
    )(
        state.reshape(planes),
        cotangent.reshape(planes),
        counts,
        edge_weights,
        node_in,
        node_out,
        biases,
    )
    outs = pl.pallas_call(
        write_out,
        out_shape=(
            jax.ShapeDtypeStruct(planes, BF16),
            jax.ShapeDtypeStruct((2, 2, H, H), F32),
            jax.ShapeDtypeStruct((2, 2 * H, H), F32),
            jax.ShapeDtypeStruct((2, H, H), F32),
            jax.ShapeDtypeStruct((2, 2, H), F32),
        ),
        in_specs=[vmem, vmem],
        out_specs=(vmem,) * 5,
        name="write_out",
    )(*outs)
    return (outs[0].reshape(shape),) + tuple(outs[1:])


def solution(mesh):
    sizes = tuple(mesh.shape[name] for name in AXES)
    grid = P("gx", "gy", "gz", None, None)
    return jax.shard_map(
        functools.partial(on_device, sizes),
        mesh=mesh,
        in_specs=(grid, grid, P("gz"), P(), P(), P(), P()),
        out_specs=(grid, P(), P(), P(), P()),
        check_vma=False,
    )
```

time: 114 us -> 95.2 us (0.84)
  Pallas kernels: 107 us -> 93.8 us
  local copies, waits for them, and re-layouts: 5.75 us -> 0 us
    pallas_call x1, Pallas kernels: 107 us -> 91.1 us  [on_device(): pl.pallas_call(functools.partial(kernel, sizes, 1.0 / math.sqrt(nodes)),...]
    unnamed x13 -> x0, local copies, waits for them, and re-layouts: 5.75 us -> none
    pallas_call x0 -> x1, Pallas kernels: none -> 2.65 us  [on_device(): pl.pallas_call(write_out, out_shape=(jax.ShapeDtypeStruct(planes, BF16),...]
where the time goes in v3:
time: 95.2 us; the launch traced here: 95.1 us
  Pallas kernels  93.8 us (99%)
  between operations  1.29 us (1%)
    pallas_call x1, Pallas kernels, on_device(): pl.pallas_call(functools.partial(kernel, sizes, 1.0 / math.sqrt(nodes)),...  91.1 us
    pallas_call x1, Pallas kernels, on_device(): pl.pallas_call(write_out, out_shape=(jax.ShapeDtypeStruct(planes, BF16),...  2.65 us

profile of v3, /device:TPU:1, one launch (start us, length us, event | category | flops | bytes accessed | tf_op | source)
XLA Modules:
  0.0 95.1 jit_solution(14929302449425694142)
XLA Ops:
  1.3 91.1 %layers.1 = (bf16[16,16,16,128]{3,2,1,0:T(8,128)(2,1)}, f32[1536,128]{1,0:T(8,128)}) custom-call(bf16[16,16,16,128]{3,2,1,0:T(8,128)(2,1)} %bitcast.3, bf16[16,16,16,128]{3,2,1,0:T(8,128)(2,1)} %bitcast.4, s32[1]{0:T(128)S(6)} %copy.12.refs_2_, bf16[2,2,128,128]{3,2,1,0:T(8,128)(2,1)} %refs_3_.1, bf16[2,256,128]{2,1,0:T(8,128)(2,1)} %refs_4_.1, ...), custom_call_target="tpu_custom_call" | custom-call | tf_op jit(solution)/shard_map/layers/pallas_call | solution.py:744
  92.4 2.6 %write_out.1 = (bf16[16,16,16,128]{3,2,1,0:T(8,128)(2,1)}, f32[2,2,128,128]{3,2,1,0:T(8,128)}, f32[2,256,128]{2,1,0:T(8,128)}, f32[2,128,128]{2,1,0:T(8,128)}, f32[2,2,128]{2,1,0:T(2,128)}) custom-call(bf16[16,16,16,128]{3,2,1,0:T(8,128)(2,1)} %get-tuple-element.12.state_in, f32[1536,128]{1,0:T(8,128)} %get-tuple-element.13.grads), custom_call_target="tpu_custom_call" | custom-call | tf_op jit(solution)/shard_map/write_out/pallas_call | solution.py:766

commit v4 on v3

--- a/solution.py
+++ b/solution.py
@@ -57,13 +57,32 @@
         return lax.rem(here[axis] + d, size[axis])
 
     def device(**moves):
-        return tuple(peer(a, moves[a] % size[a]) if a in moves else here[a] for a in AXES)
+        def place(a):
+            if a not in moves:
+                return here[a]
+            d = moves[a]
+            return peer(a, d % size[a] if isinstance(d, int) else d)
+
+        return tuple(place(a) for a in AXES)
+
+    def each(low, high, todo):
+        def step(i, _):
+            todo(i)
+            return 0
+
+        lax.fori_loop(low, high, step, 0)
 
     barrier = pltpu.get_barrier_semaphore()
-    partners = [device(**{a: d}) for a in AXES for d in range(1, size[a])]
-    partners += [device(gy=dy, gz=dz) for dy in (-1, 1) for dz in (-1, 1)]
-    for q in partners:
-        pl.semaphore_signal(barrier, inc=1, device_id=q, device_id_type=MESH)
+
+    def greet(**moves):
+        pl.semaphore_signal(barrier, inc=1, device_id=device(**moves), device_id_type=MESH)
+
+    for a in AXES:
+        each(1, size[a], lambda d, a=a: greet(**{a: d}))
+    for dy in (-1, 1):
+        for dz in (-1, 1):
+            greet(gy=dy, gz=dz)
+    greeted = n_x + n_y + n_z - 3 + 4
     load = pltpu.make_async_copy(cotangent_hbm, cotangent, load_sem.at[0])
     load.start()
 
@@ -132,13 +151,16 @@
         u, row = place
         units[u][0][row + shift : row + shift + value.shape[0]] += value
 
-    def steps(order, body, before=None, after=None):
+    def steps(order, body, before=None, after=None, groups=None, sent=(2, 4, 6)):
         before, after = before or {}, after or {}
 
         def step(i, _):
             for k, todo in before.items():
                 pl.when(i == k)(todo)
             body(order(i))
+            if groups is not None:
+                now = functools.reduce(jnp.logical_or, [i == k for k in sent])
+                pl.when(now)(lambda: start(group_copies(groups, lax.div(i + 1, 2), 4)))
             for k, todo in after.items():
                 pl.when(i == k)(todo)
             return 0
@@ -251,10 +273,10 @@
     def wait_x(e):
         wait(field.at[pl.ds(0, 2)], x_in.at[e], (ex_send.at[e], ex_recv.at[e]), len(GROUPS))
 
-    def group_copies(e, g):
+    def group_copies(e, g, planes):
         sem = (ex_send.at[e], ex_recv.at[e])
-        first = 32 if g == 0 else 0
-        n = 32 * (GROUPS[g][1] - GROUPS[g][0])
+        first = 0 if planes == 4 or g else 32
+        n = 16 * planes
 
         def one_copy(src, dst, count, to):
             return remote(
@@ -311,9 +333,6 @@
     def send_x(e):
         return lambda: start(x_copies(e))
 
-    def send(e, g):
-        return lambda: start(group_copies(e, g))
-
     def take(e, g):
         return lambda: wait_group(e, g)
 
@@ -323,7 +342,7 @@
             field[0] = field[0] + x_in[e, 0] * left["gx"]
             field[15] = field[15] + x_in[e, 1] * right["gx"]
             pack(e, 0)
-            start(group_copies(e, 0))
+            start(group_copies(e, 0, 2))
 
         return run
 
@@ -332,10 +351,10 @@
         field[7] = joint
         field[8] = joint
         pack(e, 7)
-        start(group_copies(e, 4))
-
-    def sends(e):
-        return {0: send_x(e), 2: send(e, 1), 4: send(e, 2), 6: many(send(e, 3), outer(e))}
+        start(group_copies(e, 4, 2))
+
+    def sends(e, *last):
+        return {0: send_x(e), 6: many(*last)} if last else {0: send_x(e)}
 
     def takes(e):
         return {0: take(e, 1), 2: take(e, 2), 4: take(e, 3), 6: take(e, 0), 7: take(e, 4)}
@@ -388,8 +407,10 @@
             put_field(t, lambda side, y0: cube(r[rows(side, y0)]))
             pack(e, t)
 
-        steps(ascending, body, after=sends(e))
+        steps(ascending, body, after=sends(e, outer(e)) if e else sends(e), groups=e)
         join_middle(e)
+        if not e:
+            outer(e)()
 
     def node(l, e, t):
         parts = []
@@ -438,21 +459,21 @@
             * (inv_yz[y0 : y0 + 4] * inv[side]),
         )
 
-    def by_fours(body):
+    def by_fours(body, low=0, high=4):
         def step(i, _):
             body(pl.ds(4 * i, 4))
             return 0
 
-        lax.fori_loop(0, 4, step, 0)
-
-    def node_grads(l, h_ref):
+        lax.fori_loop(low, high, step, 0)
+
+    def node_grads(l, h_ref, low=0, high=4):
         def body(at):
             d = flat(d_now[at])
             add_grad(at_out[l], 0, mm_rows(flat(active[l, at]), flat(g_now[at])))
             add_grad(at_in[l], 0, mm_rows(flat(h_ref[at]), d))
             add_grad(at_in[l], H, mm_rows(flat(agg[l, at]), d))
 
-        by_fours(body)
+        by_fours(body, low, high)
 
     def first_grad(l, h_ref):
         by_fours(lambda at: add_grad(at_one[l], 0, mm_rows(flat(h_ref[at]), flat(p_now[at]))))
@@ -494,11 +515,13 @@
             for y0, part in zip(STARTS, out):
                 p_now[plane(t, side), y0 : y0 + 4] = part
             parts += [flat(part) for part in out]
-        back = jnp.concatenate(parts, 0)
+        return jnp.concatenate(parts, 0)
+
+    def state_back(l, t, back):
         held = jnp.concatenate([flat(dh[plane(t, side)]) for side in SIDES], 0)
-        return (held + mm(back, w_one_t[l])).astype(BF16), back
-
-    def stage_copies(u, stage):
+        return (held + mm(back, w_one_t[l])).astype(BF16)
+
+    def start_stage(u, stage):
         (buf, red_y, sum_y, red_x, sum_x, red_z, sum_z, gat_x, gat_y, send_sem, recv_sem) = units[u]
         sem = (send_sem, recv_sem)
         part_y, part_x = UNITS[u] // n_y, UNITS[u] // n_y // n_x
@@ -506,27 +529,27 @@
         def part(index, rows):
             return pl.ds(pl.multiple_of(index * rows, 8), rows)
 
-        if stage == 0:
-            return [
-                remote(buf.at[part(peer("gy", d), part_y)], red_y.at[d - 1], sem, 0, device(gy=d))
-                for d in range(1, n_y)
-            ]
-        if stage == 1:
-            return [
-                remote(sum_y.at[part(peer("gx", d), part_x)], red_x.at[d - 1], sem, 1, device(gx=d))
-                for d in range(1, n_x)
-            ]
-        if stage == 2:
-            return [remote(sum_x, red_z.at[i_z], sem, 2, device(gz=d)) for d in range(1, n_z)]
-        if stage == 3:
-            return [
-                remote(sum_z, gat_x.at[part(i_x, part_x)], sem, 3, device(gx=d))
-                for d in range(1, n_x)
-            ]
-        return [
-            remote(gat_x, gat_y.at[part(i_y, part_y)], sem, 4, device(gy=d))
-            for d in range(1, n_y)
-        ]
+        def to_z(d):
+            remote(sum_x, red_z.at[i_z], sem, stage, device(gz=d)).start()
+
+        def scatter_y(d):
+            src = buf.at[part(peer("gy", d), part_y)]
+            remote(src, red_y.at[d - 1], sem, 0, device(gy=d)).start()
+
+        def scatter_x(d):
+            src = sum_y.at[part(peer("gx", d), part_x)]
+            remote(src, red_x.at[d - 1], sem, 1, device(gx=d)).start()
+
+        def gather_x(d):
+            remote(sum_z, gat_x.at[part(i_x, part_x)], sem, 3, device(gx=d)).start()
+
+        def gather_y(d):
+            remote(gat_x, gat_y.at[part(i_y, part_y)], sem, 4, device(gy=d)).start()
+
+        n, todo = (
+            (n_y, scatter_y), (n_x, scatter_x), (n_z, to_z), (n_x, gather_x), (n_y, gather_y)
+        )[stage]
+        each(1, n, todo)
 
     def wait_stage(u, stage):
         (buf, red_y, sum_y, red_x, sum_x, red_z, sum_z, gat_x, gat_y, send_sem, recv_sem) = units[u]
@@ -572,7 +595,7 @@
             if stage == 4:
                 gat_y[mine_y] = gat_x[...]
             if stage < 5:
-                start(stage_copies(u, stage))
+                start_stage(u, stage)
 
         return run
 
@@ -588,7 +611,7 @@
             ref[plane(t, side)] = cube(x[256 * side : 256 * side + 256])
 
     steps(ascending, lambda t: put_first(0, t, two(state, t)))
-    pl.semaphore_wait(barrier, len(partners))
+    pl.semaphore_wait(barrier, greeted)
     messages(0, 0)
 
     def middle(t):
@@ -613,70 +636,61 @@
         first_third,
         last,
         before={0: take(1, 1), 2: take(1, 0), 3: take(1, 2), 5: take(1, 3), 7: take(1, 4)},
-        after={1: send(2, 1), 2: send_x(2), 4: send(2, 2), 6: many(send(2, 3), outer(2))},
+        after={2: send_x(2)},
+        groups=2,
+        sent=(1, 4, 6),
     )
     join_middle(2)
-    node_grads(1, h_one)
+    node_grads(1, h_one, 0, 3)
+    outer(2)()
+    node_grads(1, h_one, 3, 4)
     edge_first(1, 2)
     reduce_step(0, 0)()
     carry[...] = jnp.zeros_like(carry)
 
     def turnover(t):
-        g, _ = edge_back(1, t)
+        g = state_back(1, t, edge_back(1, t))
         saved = [slope_n[plane(t, side), y0 : y0 + 4] for side in SIDES for y0 in STARTS]
         node_back(0, t, g, [flat(x) for x in saved])
         pack(3, t)
 
-    after = sends(3)
-    after[5] = reduce_step(0, 1)
-    steps(ascending, turnover, after=after)
+    steps(ascending, turnover, after=sends(3, reduce_step(0, 1)), groups=3)
     join_middle(3)
+    outer(3)()
     first_grad(1, h_one)
     node_grads(0, state)
     reduce_step(1, 0)()
-    reduce_step(0, 2)()
     finish_bias(0, 1)
     finish_bias(1, 0)
     finish_bias(1, 1)
     edge_first(0, 3)
     reduce_step(2, 0)()
-    reduce_step(1, 1)()
-    reduce_step(0, 3)()
+    reduce_step(0, 2)()
     carry[...] = jnp.zeros_like(carry)
 
     def final(t):
-        g, back = edge_back(0, t)
-        put_two(state_grad, t, g)
+        back = edge_back(0, t)
+        put_two(state_grad, t, state_back(0, t, back))
         add_grad(at_one[0], 0, mm_rows(two(state, t), back))
 
-    steps(
-        ascending,
-        final,
-        after={6: many(reduce_step(1, 2), reduce_step(0, 4), reduce_step(2, 1))},
-    )
+    steps(ascending, final, after={3: reduce_step(1, 1), 6: reduce_step(2, 1)})
     finish_bias(0, 0)
     reduce_step(3, 0)()
+    reduce_step(0, 3)()
     store = pltpu.make_async_copy(state_grad, state_grad_hbm, load_sem.at[1])
     store.start()
-    reduce_step(3, 1)()
-    reduce_step(1, 3)()
-    reduce_step(2, 2)()
-    reduce_step(3, 2)()
-    reduce_step(0, 5)()
-    reduce_step(1, 4)()
-    reduce_step(2, 3)()
-    reduce_step(3, 3)()
-    reduce_step(1, 5)()
-    reduce_step(2, 4)()
-    reduce_step(2, 5)()
+    for u, stage in (
+        (3, 1), (1, 2), (2, 2), (0, 4), (3, 2), (2, 3), (1, 3), (0, 5), (3, 3), (2, 4), (1, 4),
+        (3, 4), (2, 5),
+    ):
+        reduce_step(u, stage)()
     row = 0
-    for u in range(len(UNITS) - 1):
+    for u, stage in ((0, None), (1, 5), (2, None), (3, 5)):
+        if stage:
+            reduce_step(u, stage)()
         grads[row : row + UNITS[u]] = units[u][8][...]
         row += UNITS[u]
     store.wait()
-    reduce_step(3, 4)()
-    reduce_step(3, 5)()
-    grads[row : row + UNITS[3]] = units[3][8][...]
 
 
 def write_out(state_in, grads, state_grad, edge_grads, node_in_grad, node_out_grad, bias_grads):

time: 95.2 us -> 89.2 us (0.937)
  Pallas kernels: 93.8 us -> 87.7 us
    pallas_call x1, Pallas kernels: 91.1 us -> 85.1 us  [on_device(): pl.pallas_call(functools.partial(kernel, sizes, 1.0 / math.sqrt(nodes)),...]
where the time goes in v4:
time: 89.2 us; the launch traced here: 89 us
  Pallas kernels  87.7 us (98%)
  between operations  1.29 us (1%)
    pallas_call x1, Pallas kernels, on_device(): pl.pallas_call(functools.partial(kernel, sizes, 1.0 / math.sqrt(nodes)),...  85.1 us
    pallas_call x1, Pallas kernels, on_device(): pl.pallas_call(write_out, out_shape=(jax.ShapeDtypeStruct(planes, BF16),...  2.65 us

profile of v4, /device:TPU:1, one launch (start us, length us, event | category | flops | bytes accessed | tf_op | source)
XLA Modules:
  0.0 89.0 jit_solution(1992010914862761883)
XLA Ops:
  1.3 85.1 %layers.1 = (bf16[16,16,16,128]{3,2,1,0:T(8,128)(2,1)}, f32[1536,128]{1,0:T(8,128)}) custom-call(bf16[16,16,16,128]{3,2,1,0:T(8,128)(2,1)} %bitcast.3, bf16[16,16,16,128]{3,2,1,0:T(8,128)(2,1)} %bitcast.4, s32[1]{0:T(128)S(6)} %copy.12.refs_2_, bf16[2,2,128,128]{3,2,1,0:T(8,128)(2,1)} %refs_3_.1, bf16[2,256,128]{2,1,0:T(8,128)(2,1)} %refs_4_.1, ...), custom_call_target="tpu_custom_call" | custom-call | tf_op jit(solution)/shard_map/layers/pallas_call | solution.py:758
  86.4 2.6 %write_out.1 = (bf16[16,16,16,128]{3,2,1,0:T(8,128)(2,1)}, f32[2,2,128,128]{3,2,1,0:T(8,128)}, f32[2,256,128]{2,1,0:T(8,128)}, f32[2,128,128]{2,1,0:T(8,128)}, f32[2,2,128]{2,1,0:T(2,128)}) custom-call(bf16[16,16,16,128]{3,2,1,0:T(8,128)(2,1)} %get-tuple-element.12.state_in, f32[1536,128]{1,0:T(8,128)} %get-tuple-element.13.grads), custom_call_target="tpu_custom_call" | custom-call | tf_op jit(solution)/shard_map/write_out/pallas_call | solution.py:780

commit v5 on v4

--- a/solution.py
+++ b/solution.py
@@ -216,7 +216,7 @@
                 else:
                     field[p, y0 : y0 + 4] = r
 
-    def edge_chunks(t, side, per_edge):
+    def edge_chunks(t, side, per_edge, bias=None):
         p = plane(t, side)
         nxt = jnp.maximum(14 - t, 8) if side else jnp.minimum(t + 1, 7)
         zero_row = jnp.zeros((1, 16, H), F32)
@@ -224,20 +224,22 @@
         for y0 in STARTS:
             ys = slice(y0, y0 + 4)
             mine = pre_a[p, ys]
+            low = mine if bias is None else mine - bias
             if side:
-                ux = per_edge(0, pre_a[nxt, ys], mine, p, y0, 4)
+                high = mine if bias is None else mine + bias
+                ux = per_edge(0, pre_a[nxt, ys], high, p, y0, 4)
                 total = ux - carry[side, ys]
             else:
-                ux = per_edge(0, mine, pre_a[nxt, ys], p, y0, 4)
+                ux = per_edge(0, low, pre_a[nxt, ys], p, y0, 4)
                 total = carry[side, ys] - ux
             carry[side, ys] = ux
             n = 3 if y0 % 8 else 4
-            uy = per_edge(1, mine[:n], pre_a[p, y0 + 1 : y0 + 1 + n], p, y0, n)
+            uy = per_edge(1, low[:n], pre_a[p, y0 + 1 : y0 + 1 + n], p, y0, n)
             arriving = jnp.concatenate([held if y0 % 8 else zero_row, uy[:3]], 0)
             held = uy[3:4] if n == 4 else None
             leaving = uy if n == 4 else jnp.concatenate([uy, zero_row], 0)
             total = total + (arriving - leaving)
-            uz = per_edge(2, mine, roll_k(mine, 7), p, y0, 4)
+            uz = per_edge(2, low, roll_k(mine, 7), p, y0, 4)
             total = total + (roll_k(uz, 1) - uz)
             out.append(total.astype(BF16))
         return out
@@ -389,7 +391,7 @@
             inner = 1.0 - flag(t == 7)
 
             def per_edge(dim, low, high, p, y0, n):
-                u, slope = act((high - low) + bias)
+                u, slope = act(high - low)
                 if dim == 0:
                     u, slope = u * inner, slope * inner
                 if dim == 2:
@@ -399,7 +401,7 @@
 
             parts = []
             for side in SIDES:
-                out = edge_chunks(t, side, per_edge)
+                out = edge_chunks(t, side, per_edge, bias)
                 for y0, part in zip(STARTS, out):
                     spread[l, plane(t, side), y0 : y0 + 4] = part
                 parts += [flat(part) for part in out]
@@ -654,9 +656,10 @@
         node_back(0, t, g, [flat(x) for x in saved])
         pack(3, t)
 
-    steps(ascending, turnover, after=sends(3, reduce_step(0, 1)), groups=3)
+    steps(ascending, turnover, after=sends(3), groups=3)
     join_middle(3)
     outer(3)()
+    reduce_step(0, 1)()
     first_grad(1, h_one)
     node_grads(0, state)
     reduce_step(1, 0)()
@@ -673,9 +676,10 @@
         put_two(state_grad, t, state_back(0, t, back))
         add_grad(at_one[0], 0, mm_rows(two(state, t), back))
 
-    steps(ascending, final, after={3: reduce_step(1, 1), 6: reduce_step(2, 1)})
+    steps(ascending, final, after={5: reduce_step(1, 1)})
     finish_bias(0, 0)
     reduce_step(3, 0)()
+    reduce_step(2, 1)()
     reduce_step(0, 3)()
     store = pltpu.make_async_copy(state_grad, state_grad_hbm, load_sem.at[1])
     store.start()

time: 89.2 us -> 88.2 us (0.989)
  Pallas kernels: 87.7 us -> 86.8 us
    pallas_call x1, Pallas kernels: 85.1 us -> 84.1 us  [on_device(): pl.pallas_call(functools.partial(kernel, sizes, 1.0 / math.sqrt(nodes)),...]
where the time goes in v5:
time: 88.2 us; the launch traced here: 88.1 us
  Pallas kernels  86.8 us (98%)
  between operations  1.29 us (1%)
    pallas_call x1, Pallas kernels, on_device(): pl.pallas_call(functools.partial(kernel, sizes, 1.0 / math.sqrt(nodes)),...  84.1 us
    pallas_call x1, Pallas kernels, on_device(): pl.pallas_call(write_out, out_shape=(jax.ShapeDtypeStruct(planes, BF16),...  2.65 us

profile of v5, /device:TPU:1, one launch (start us, length us, event | category | flops | bytes accessed | tf_op | source)
XLA Modules:
  0.0 88.1 jit_solution(12357446576855253547)
XLA Ops:
  1.3 84.1 %layers.1 = (bf16[16,16,16,128]{3,2,1,0:T(8,128)(2,1)}, f32[1536,128]{1,0:T(8,128)}) custom-call(bf16[16,16,16,128]{3,2,1,0:T(8,128)(2,1)} %bitcast.3, bf16[16,16,16,128]{3,2,1,0:T(8,128)(2,1)} %bitcast.4, s32[1]{0:T(128)S(6)} %copy.12.refs_2_, bf16[2,2,128,128]{3,2,1,0:T(8,128)(2,1)} %refs_3_.1, bf16[2,256,128]{2,1,0:T(8,128)(2,1)} %refs_4_.1, ...), custom_call_target="tpu_custom_call" | custom-call | tf_op jit(solution)/shard_map/layers/pallas_call | solution.py:762
  85.4 2.6 %write_out.1 = (bf16[16,16,16,128]{3,2,1,0:T(8,128)(2,1)}, f32[2,2,128,128]{3,2,1,0:T(8,128)}, f32[2,256,128]{2,1,0:T(8,128)}, f32[2,128,128]{2,1,0:T(8,128)}, f32[2,2,128]{2,1,0:T(2,128)}) custom-call(bf16[16,16,16,128]{3,2,1,0:T(8,128)(2,1)} %get-tuple-element.12.state_in, f32[1536,128]{1,0:T(8,128)} %get-tuple-element.13.grads), custom_call_target="tpu_custom_call" | custom-call | tf_op jit(solution)/shard_map/write_out/pallas_call | solution.py:784

commit v6 on v5

--- a/solution.py
+++ b/solution.py
@@ -289,8 +289,8 @@
         for f in (0, 1):
             move = 2 * f - 1
             src, dst = 64 * f + first, 64 * (1 - f) + first
+            copies.insert(f, one_copy(128 + src, 128 + dst, n, device(gz=move)))
             copies.append(one_copy(src, dst, n, device(gy=move)))
-            copies.append(one_copy(128 + src, 128 + dst, n, device(gz=move)))
             for fy in (0, 1):
                 src, dst = 256 + 8 * (2 * f + fy), 256 + 8 * (3 - 2 * f - fy)
                 copies.append(one_copy(src, dst, 8, device(gy=2 * fy - 1, gz=move)))

time: 88.2 us -> 87.9 us (level)
  no operation moved by 1% of the time
where the time goes in v6:
time: 87.9 us; the launch traced here: 87.8 us
  Pallas kernels  86.5 us (98%)
  between operations  1.29 us (1%)
    pallas_call x1, Pallas kernels, on_device(): pl.pallas_call(functools.partial(kernel, sizes, 1.0 / math.sqrt(nodes)),...  83.8 us
    pallas_call x1, Pallas kernels, on_device(): pl.pallas_call(write_out, out_shape=(jax.ShapeDtypeStruct(planes, BF16),...  2.65 us

profile of v6, /device:TPU:1, one launch (start us, length us, event | category | flops | bytes accessed | tf_op | source)
XLA Modules:
  0.0 87.8 jit_solution(5174265650823407072)
XLA Ops:
  1.3 83.8 %layers.1 = (bf16[16,16,16,128]{3,2,1,0:T(8,128)(2,1)}, f32[1536,128]{1,0:T(8,128)}) custom-call(bf16[16,16,16,128]{3,2,1,0:T(8,128)(2,1)} %bitcast.3, bf16[16,16,16,128]{3,2,1,0:T(8,128)(2,1)} %bitcast.4, s32[1]{0:T(128)S(6)} %copy.12.refs_2_, bf16[2,2,128,128]{3,2,1,0:T(8,128)(2,1)} %refs_3_.1, bf16[2,256,128]{2,1,0:T(8,128)(2,1)} %refs_4_.1, ...), custom_call_target="tpu_custom_call" | custom-call | tf_op jit(solution)/shard_map/layers/pallas_call | solution.py:762
  85.1 2.6 %write_out.1 = (bf16[16,16,16,128]{3,2,1,0:T(8,128)(2,1)}, f32[2,2,128,128]{3,2,1,0:T(8,128)}, f32[2,256,128]{2,1,0:T(8,128)}, f32[2,128,128]{2,1,0:T(8,128)}, f32[2,2,128]{2,1,0:T(2,128)}) custom-call(bf16[16,16,16,128]{3,2,1,0:T(8,128)(2,1)} %get-tuple-element.12.state_in, f32[1536,128]{1,0:T(8,128)} %get-tuple-element.13.grads), custom_call_target="tpu_custom_call" | custom-call | tf_op jit(solution)/shard_map/write_out/pallas_call | solution.py:784
